TPU v7x, 32 devices: a whole 2x2x4 slice. The times are simulated.
32 devices in a mesh: gx: 4 (over z), gy: 4 (over x, core), gz: 2 (over y).
Axes of the slice: x: 2, y: 2, z: 4, core: 2. Of those that a mesh axis runs over, the one named last changes fastest.
Arguments:
- order_real: float32 [32, 256, 512], P('gz', 'gx', 'gy'), may hold values from -2.5 to 2.5
- order_imag: float32 [32, 256, 512], P('gz', 'gx', 'gy'), may hold values from -2.5 to 2.5
- phase_z: float32 [32, 256, 512], P('gz', 'gx', 'gy'), may hold values from -3.140625 to 3.140625
- phase_x: float32 [32, 256, 512], P('gz', 'gx', 'gy'), may hold values from -3.140625 to 3.140625
- phase_y: float32 [32, 256, 512], P('gz', 'gx', 'gy'), may hold values from -3.140625 to 3.140625
- material: int32 [32, 256, 512], P('gz', 'gx', 'gy'), may hold values from 0 to 7
- levels: float32 [8], replicated, may hold values from -0.5 to 1.5
Outputs:
- final_real: float32 [32, 256, 512], P('gz', 'gx', 'gy')
- final_imag: float32 [32, 256, 512], P('gz', 'gx', 'gy')
- circulation: float32 [32, 256, 512], P('gz', ('gx', 'gy'))
- current_flux: float32 [32, 256, 512], P('gz', ('gx', 'gy'))
All inputs are finite; a program needn't handle non-finite values.
Results may differ from a plain program's by a relative error of at most 0.0003.
Values sent between devices are 32-bit elements; how exact they have to be, the bound alone decides.
A program may use at most 64 MiB of HBM per device.

v0:
```python
import jax
import jax.numpy as jnp
from jax import lax
from jax.sharding import PartitionSpec as P

STEPS = 2
LEVELS = 8


time_step = 0.15


def passed_along(block, axis, distance):
    devices = range(lax.axis_size(axis))
    route = [(i - distance, i) for i in devices if i - distance in devices]
    return lax.ppermute(block, axis, route)


def extended(x, sides, width):
    for axis, dim in sides:
        size, length = (lax.axis_size(axis), x.shape[dim])
        up = [(i, (i + 1) % size) for i in range(size - 1)]
        down = [(j, i) for i, j in up]
        last = lax.slice_in_dim(x, length - width, length, axis=dim)
        initial = lax.slice_in_dim(x, 0, width, axis=dim)
        before = lax.ppermute(last, axis, up)
        after = lax.ppermute(initial, axis, down)
        x = jnp.concatenate([before, x, after], axis=dim)
    return x


def prefix(value, axis, join, neutral):
    count, mine = (lax.axis_size(axis), lax.axis_index(axis))
    pieces = lax.all_gather(value, axis)
    subtotal = jnp.full_like(value, 0) + jnp.asarray(neutral, value.dtype)

    def step(position, subtotal):
        longer = join(subtotal, pieces[position])
        return jnp.where(position < mine, longer, subtotal)

    return lax.fori_loop(0, count - 1, step, subtotal)


def inner(values, direction, offset):
    slicer = [slice(1, length - 1) for length in values.shape]
    length = values.shape[direction]
    slicer[direction] = slice(1 + offset, length - 1 + offset)
    return values[tuple(slicer)]


def advance(real_part, imag_part, cosines, sine_parts, epsilon):
    centre_real = inner(real_part, 0, 0)
    centre_imag = inner(imag_part, 0, 0)
    lap_real = -6.0 * centre_real
    lap_imag = -6.0 * centre_imag
    for direction in range(3):
        cosine = inner(cosines[direction], direction, 0)
        sine_part = inner(sine_parts[direction], direction, 0)
        ahead_real = inner(real_part, direction, 1)
        ahead_imag = inner(imag_part, direction, 1)
        lap_real = lap_real + cosine * ahead_real - sine_part * ahead_imag
        lap_imag = lap_imag + cosine * ahead_imag + sine_part * ahead_real
        cosine = inner(cosines[direction], direction, -1)
        sine_part = inner(sine_parts[direction], direction, -1)
        behind_real = inner(real_part, direction, -1)
        behind_imag = inner(imag_part, direction, -1)
        lap_real = lap_real + cosine * behind_real + sine_part * behind_imag
        lap_imag = lap_imag + cosine * behind_imag - sine_part * behind_real
    density = centre_real * centre_real + centre_imag * centre_imag
    new_real = centre_real + time_step * ((epsilon - density) * centre_real + lap_real)
    new_imag = centre_imag + time_step * ((epsilon - density) * centre_imag + lap_imag)
    return (new_real, new_imag)


def current(first_real, first_imag, second_real, second_imag, phase):
    cosine = jnp.cos(phase)
    sine_part = jnp.sin(phase)
    turned_real = cosine * second_real - sine_part * second_imag
    turned_imag = cosine * second_imag + sine_part * second_real
    return first_real * turned_imag - first_imag * turned_real


def analyse(upper_real, upper_imag, phase_along_x, phase_along_y):
    rows = phase_along_x.shape[1]
    cols = phase_along_y.shape[2]
    current_x = current(
        upper_real[:, :rows, :],
        upper_imag[:, :rows, :],
        upper_real[:, 1:, :],
        upper_imag[:, 1:, :],
        phase_along_x,
    )
    current_y = current(
        upper_real[:, :, :cols],
        upper_imag[:, :, :cols],
        upper_real[:, :, 1:],
        upper_imag[:, :, 1:],
        phase_along_y,
    )
    circulation = (
        current_x[:, :, :cols] + current_y[:, 1:, :] - current_x[:, :, 1:] - current_y[:, :rows, :]
    )
    return (circulation, current_x[:, :, :cols])


def prefix_sum(values):
    length = values.shape[-1]
    width = 128
    blocks = values.reshape(values.shape[:-1] + (length // width, width))
    triangle = (
        lax.broadcasted_iota(jnp.int32, (width, width), 0)
        <= lax.broadcasted_iota(jnp.int32, (width, width), 1)
    ).astype(jnp.float32)
    within = jnp.einsum("abcd,de->abce", blocks, triangle, precision=lax.Precision.HIGHEST)
    totals = within[..., -1]
    offsets = jnp.cumsum(totals, axis=-1) - totals
    return (within + offsets[..., None]).reshape(values.shape)


def extend_below(phase, below, direction):
    joined = jnp.concatenate([below, phase], axis=direction)
    widths = [(1, 1), (1, 1), (1, 1)]
    widths[direction] = (0, 1)
    return jnp.pad(joined, widths)


def shards(order_real, order_imag, phase_z, phase_x, phase_y, material, levels):
    epsilon = jnp.zeros(order_real.shape, jnp.float32)
    for level in range(LEVELS):
        epsilon = epsilon + jnp.where(material == level, levels[level], 0.0)
    below_z = passed_along(phase_z[-1:], "gz", 1)
    below_x = passed_along(phase_x[:, -1:], "gx", 1)
    below_y = passed_along(phase_y[:, :, -1:], "gy", 1)
    link_halo = [
        extend_below(phase_z, below_z, 0),
        extend_below(phase_x, below_x, 1),
        extend_below(phase_y, below_y, 2),
    ]
    cosines = [jnp.cos(phase) for phase in link_halo]
    sine_parts = [jnp.sin(phase) for phase in link_halo]
    real_part, imag_part = (order_real, order_imag)
    for turn in range(STEPS):
        padded = (
            extended(real_part, (("gx", 1), ("gy", 2), ("gz", 0)), 1),
            extended(imag_part, (("gx", 1), ("gy", 2), ("gz", 0)), 1),
        )
        real_part, imag_part = advance(padded[0], padded[1], cosines, sine_parts, epsilon)
    edges = (
        extended(real_part, (("gx", 1), ("gy", 2)), 1),
        extended(imag_part, (("gx", 1), ("gy", 2)), 1),
    )
    upper_real = edges[0][:, 1:, 1:]
    upper_imag = edges[1][:, 1:, 1:]
    ahead_x = passed_along(phase_x[:, :, :1], "gy", -1)
    ahead_y = passed_along(phase_y[:, :1, :], "gx", -1)
    phase_along_x = jnp.concatenate([phase_x, ahead_x], axis=2)
    phase_along_y = jnp.concatenate([phase_y, ahead_y], axis=1)
    circulation, current_x = analyse(upper_real, upper_imag, phase_along_x, phase_along_y)
    local_flux = prefix_sum(current_x)
    totals = local_flux[:, :, -1]
    before = prefix(totals, "gy", lambda earlier, later: earlier + later, jnp.zeros_like(totals))
    local_flux = local_flux + before[:, :, None]
    circulation, current_flux = (
        lax.all_to_all(circulation, "gy", split_axis=1, concat_axis=2, tiled=True),
        lax.all_to_all(local_flux, "gy", split_axis=1, concat_axis=2, tiled=True),
    )
    return (real_part, imag_part, circulation, current_flux)


def solution(mesh):
    in_specs = (
        P("gz", "gx", "gy"),
        P("gz", "gx", "gy"),
        P("gz", "gx", "gy"),
        P("gz", "gx", "gy"),
        P("gz", "gx", "gy"),
        P("gz", "gx", "gy"),
        P(),
    )
    out_specs = (
        P("gz", "gx", "gy"),
        P("gz", "gx", "gy"),
        P("gz", ("gx", "gy"), None),
        P("gz", ("gx", "gy"), None),
    )
    return jax.shard_map(shards, mesh=mesh, in_specs=in_specs, out_specs=out_specs, check_vma=False)
```

profile of v0, /device:TPU:0, one launch (start us, length us, event | category | flops | bytes accessed | tf_op | source)
XLA Modules:
  0.0 249.5 jit_solution(15184229427270982170)
XLA Ops:
  2.0 2.4 collective-permute-start.14
  5.3 4.3 %collective-permute-start.13 = (f32[16,1,128]{2,1,0:T(1,128)S(1)}, f32[16,1,128]{2,1,0:T(1,128)S(1)}, u32[]{:S(2)}, u32[]{:S(2)}) collective-permute-start(f32[16,1,128]{2,1,0:T(1,128)S(1)} %slice.357), channel_id=1, source_target_pairs={{0,8},{8,16},{16,24},{1,9},{9,17},{17,25},{2,10},{10,18},{18,26},{... | collective-permute-start | bytes 24584 | tf_op jit(solution)/shard_map/ppermute | solution.py:16
  11.0 3.4 %collective-permute-start = (f32[1,64,128]{2,1,0:T(8,128)}, f32[1,64,128]{2,1,0:T(8,128)S(1)}, u32[]{:S(2)}, u32[]{:S(2)}) collective-permute-start(f32[1,64,128]{2,1,0:T(8,128)} %slice.336), channel_id=1, source_target_pairs={{0,1},{2,3},{4,5},{6,7},{8,9},{10,11},{12,13},{14,15},{16,17},{18,... | collective-permute-start | bytes 98312 | tf_op jit(solution)/shard_map/ppermute | solution.py:16
  22.6 5.3 %collective-permute-start.1 = (f32[16,1,128]{2,1,0:T(1,128)S(1)}, f32[16,1,128]{2,1,0:T(1,128)S(1)}, u32[]{:S(2)}, u32[]{:S(2)}) collective-permute-start(f32[16,1,128]{2,1,0:T(1,128)S(1)} %get-tuple-element.139), channel_id=1, source_target_pairs={{0,8},{8,16},{16,24},{1,9},{9,17},{17,25},{2,10},{10,18},{18,26},{... | collective-permute-start | bytes 24584 | tf_op jit(solution)/shard_map/ppermute | solution.py:26
  27.9 6.4 %fusion.22 = (f32[18,66,130]{2,1,0:T(8,128)S(1)}, f32[18,66,130]{2,1,0:T(8,128)S(1)}) fusion(f32[16,64,128]{2,1,0:T(8,128)S(1)} %copy-done.29, f32[16,64,1]{2,1,0:T(8,128)} %copy-done.34), kind=kLoop, calls=%fused_computation.151 | loop fusion | flops 2471040 | bytes 1763904 | tf_op jit(solution)/shard_map/cos | solution.py:139
  34.3 3.9 %collective-permute-start.6 = (f32[16,1,128]{2,1,0:T(1,128)S(1)}, f32[16,1,128]{2,1,0:T(1,128)S(1)}, u32[]{:S(2)}, u32[]{:S(2)}) collective-permute-start(f32[16,1,128]{2,1,0:T(1,128)S(1)} %get-tuple-element.137), channel_id=1, source_target_pairs={{0,8},{8,16},{16,24},{1,9},{9,17},{17,25},{2,10},{10,18},{18,26},{... | collective-permute-start | bytes 24584 | tf_op jit(solution)/shard_map/ppermute | solution.py:26
  47.6 3.8 %collective-permute-start.3 = (f32[16,66,1]{1,0,2:T(8,128)S(1)}, f32[16,66,1]{1,0,2:T(8,128)S(1)}, u32[]{:S(2)}, u32[]{:S(2)}) collective-permute-start(f32[16,66,1]{1,0,2:T(8,128)S(1)} %copy.15), channel_id=1, source_target_pairs={{0,2},{2,4},{4,6},{1,3},{3,5},{5,7},{8,10},{10,12},{12,14},{9,11},... | collective-permute-start | bytes 12680 | tf_op jit(solution)/shard_map/ppermute | solution.py:26
  51.4 8.2 %fusion.18 = (f32[18,66,130]{2,1,0:T(8,128)}, f32[18,66,130]{2,1,0:T(8,128)}) fusion(f32[16,64,128]{2,1,0:T(8,128)} %param.12, f32[16,1,128]{2,1,0:T(1,128)S(1)} %collective-permute-done.13), kind=kLoop, calls=%fused_computation.127 | loop fusion | flops 2471040 | bytes 1768000 | tf_op jit(solution)/shard_map/cos | solution.py:139
  59.9 4.2 %collective-permute-start.8 = (f32[16,66,1]{1,0,2:T(8,128)S(1)}, f32[16,66,1]{1,0,2:T(8,128)}, u32[]{:S(2)}, u32[]{:S(2)}) collective-permute-start(f32[16,66,1]{1,0,2:T(8,128)S(1)} %copy.19), channel_id=1, source_target_pairs={{0,2},{2,4},{4,6},{1,3},{3,5},{5,7},{8,10},{10,12},{12,14},{9,11},... | collective-permute-start | bytes 12680 | tf_op jit(solution)/shard_map/ppermute | solution.py:26
  67.9 1.8 copy.22
  69.7 1.8 copy.21
  73.9 4.6 %collective-permute-start.11 = (f32[1,66,130]{2,1,0:T(8,128)S(1)}, f32[1,66,130]{2,1,0:T(8,128)S(1)}, u32[]{:S(2)}, u32[]{:S(2)}) collective-permute-start(f32[1,66,130]{2,1,0:T(8,128)S(1)} %get-tuple-element.113), channel_id=1, source_target_pairs={{0,1},{2,3},{4,5},{6,7},{8,9},{10,11},{12,13},{14,15},{16,17},{18,... | collective-permute-start | bytes 102968 | tf_op jit(solution)/shard_map/ppermute | solution.py:26
  80.2 6.4 %fusion.16 = (f32[18,66,130]{2,1,0:T(8,128)S(1)}, f32[18,66,130]{2,1,0:T(8,128)S(1)}) fusion(f32[16,64,128]{2,1,0:T(8,128)} %param.11, f32[1,64,128]{2,1,0:T(8,128)S(1)} %collective-permute-done), kind=kLoop, calls=%fused_computation.125 | loop fusion | flops 2471040 | bytes 1792576 | tf_op jit(solution)/shard_map/cos | solution.py:139
  88.1 12.2 %multiply_add_fusion.3 = f32[16,64,128]{2,1,0:T(8,128)S(1)} fusion(f32[16,64,128]{2,1,0:T(8,128)S(1)} %copy-done.19, f32[16,64,128]{2,1,0:T(8,128)} %param.10, f32[18,66,130]{2,1,0:T(8,128)S(1)} %get-tuple-element.116, f32[18,66,130]{2,1,0:T(8,128)S(1)} %get-tuple-element.115, f32[18,66,130]{2,1,0:T(8,128)S(1)} %copy-done.2, f32[18,66,130]{2,1,0:T(8,128)S(1)} %copy-done, ...), kind=kLoop, calls=%fused_computation.118 | loop fusion | flops 12058624 | bytes 8575584 | tf_op jit(solution)/shard_map/add | solution.py:70
  101.6 5.2 %collective-permute-start.15 = (f32[16,1,128]{2,1,0:T(1,128)S(1)}, f32[16,1,128]{2,1,0:T(1,128)S(1)}, u32[]{:S(2)}, u32[]{:S(2)}) collective-permute-start(f32[16,1,128]{2,1,0:T(1,128)S(1)} %get-tuple-element.135), channel_id=1, source_target_pairs={{0,8},{8,16},{16,24},{1,9},{9,17},{17,25},{2,10},{10,18},{18,26},{... | collective-permute-start | bytes 24584 | tf_op jit(solution)/shard_map/ppermute | solution.py:26
  106.8 10.7 %multiply_add_fusion.2 = f32[16,64,128]{2,1,0:T(8,128)S(1)} fusion(f32[16,64,128]{2,1,0:T(8,128)S(1)} %copy-done.21, f32[16,64,128]{2,1,0:T(8,128)S(1)} %copy-done.19, f32[18,66,130]{2,1,0:T(8,128)S(1)} %get-tuple-element.116, f32[18,66,130]{2,1,0:T(8,128)S(1)} %get-tuple-element.115, f32[18,66,130]{2,1,0:T(8,128)S(1)} %copy-done.2, ...), kind=kLoop, calls=%fused_computation.117 | loop fusion | flops 12058624 | bytes 8575584 | tf_op jit(solution)/shard_map/add | solution.py:71
  118.9 4.6 %collective-permute-start.20 = (f32[16,1,128]{2,1,0:T(1,128)S(1)}, f32[16,1,128]{2,1,0:T(1,128)S(1)}, u32[]{:S(2)}, u32[]{:S(2)}) collective-permute-start(f32[16,1,128]{2,1,0:T(1,128)S(1)} %get-tuple-element.133), channel_id=1, source_target_pairs={{0,8},{8,16},{16,24},{1,9},{9,17},{17,25},{2,10},{10,18},{18,26},{... | collective-permute-start | bytes 24584 | tf_op jit(solution)/shard_map/ppermute | solution.py:26
  128.8 3.0 %collective-permute-start.17 = (f32[16,66,1]{1,0,2:T(8,128)S(1)}, f32[16,66,1]{1,0,2:T(8,128)S(1)}, u32[]{:S(2)}, u32[]{:S(2)}) collective-permute-start(f32[16,66,1]{1,0,2:T(8,128)S(1)} %copy.27), channel_id=1, source_target_pairs={{0,2},{2,4},{4,6},{1,3},{3,5},{5,7},{8,10},{10,12},{12,14},{9,11},... | collective-permute-start | bytes 12680 | tf_op jit(solution)/shard_map/ppermute | solution.py:26
  137.2 4.1 %collective-permute-start.22 = (f32[16,66,1]{1,0,2:T(8,128)S(1)}, f32[16,66,1]{1,0,2:T(8,128)S(1)}, u32[]{:S(2)}, u32[]{:S(2)}) collective-permute-start(f32[16,66,1]{1,0,2:T(8,128)S(1)} %copy.31), channel_id=1, source_target_pairs={{0,2},{2,4},{4,6},{1,3},{3,5},{5,7},{8,10},{10,12},{12,14},{9,11},... | collective-permute-start | bytes 12680 | tf_op jit(solution)/shard_map/ppermute | solution.py:26
  151.7 4.5 %collective-permute-start.25 = (f32[1,66,130]{2,1,0:T(8,128)}, f32[1,66,130]{2,1,0:T(8,128)S(1)}, u32[]{:S(2)}, u32[]{:S(2)}) collective-permute-start(f32[1,66,130]{2,1,0:T(8,128)} %get-tuple-element.109), channel_id=1, source_target_pairs={{0,1},{2,3},{4,5},{6,7},{8,9},{10,11},{12,13},{14,15},{16,17},{18,... | collective-permute-start | bytes 102968 | tf_op jit(solution)/shard_map/ppermute | solution.py:26
  157.6 1.9 constant_dynamic-update-slice_fusion
  161.2 17.3 %multiply_add_fusion.1 = f32[16,64,128]{2,1,0:T(8,128)S(1)} fusion(f32[16,64,128]{2,1,0:T(8,128)} %copy-done.8, f32[16,64,128]{2,1,0:T(8,128)S(1)} %multiply_add_fusion.2, f32[18,66,130]{2,1,0:T(8,128)S(1)} %get-tuple-element.116, f32[18,66,130]{2,1,0:T(8,128)S(1)} %get-tuple-element.115, f32[18,66,130]{2,1,0:T(8,128)} %get-tuple-element.128, ...), kind=kLoop, calls=%fused_computation.115 | loop fusion | flops 12058624 | bytes 8575584 | tf_op jit(solution)/shard_map/add | solution.py:70
  179.8 4.5 %collective-permute-start.27 = (f32[16,1,128]{2,1,0:T(1,128)S(1)}, f32[16,1,128]{2,1,0:T(1,128)S(1)}, u32[]{:S(2)}, u32[]{:S(2)}) collective-permute-start(f32[16,1,128]{2,1,0:T(1,128)S(1)} %get-tuple-element.131), channel_id=1, source_target_pairs={{0,8},{8,16},{16,24},{1,9},{9,17},{17,25},{2,10},{10,18},{18,26},{... | collective-permute-start | bytes 24584 | tf_op jit(solution)/shard_map/ppermute | solution.py:26
  184.5 9.8 %multiply_add_fusion = f32[16,64,128]{2,1,0:T(8,128)S(1)} fusion(f32[16,64,128]{2,1,0:T(8,128)S(1)} %multiply_add_fusion.2, f32[16,64,128]{2,1,0:T(8,128)S(1)} %copy-done.9, f32[18,66,130]{2,1,0:T(8,128)S(1)} %get-tuple-element.116, f32[18,66,130]{2,1,0:T(8,128)S(1)} %get-tuple-element.115, f32[18,66,130]{2,1,0:T(8,128)S(1)} %copy-done.3, ...), kind=kLoop, calls=%fused_computation.114 | loop fusion | flops 12058624 | bytes 8575584 | tf_op jit(solution)/shard_map/add | solution.py:71
  195.6 4.5 %collective-permute-start.31 = (f32[16,1,128]{2,1,0:T(1,128)S(1)}, f32[16,1,128]{2,1,0:T(1,128)S(1)}, u32[]{:S(2)}, u32[]{:S(2)}) collective-permute-start(f32[16,1,128]{2,1,0:T(1,128)S(1)} %get-tuple-element.129), channel_id=1, source_target_pairs={{0,8},{8,16},{16,24},{1,9},{9,17},{17,25},{2,10},{10,18},{18,26},{... | collective-permute-start | bytes 24584 | tf_op jit(solution)/shard_map/ppermute | solution.py:26
  204.9 1.9 collective-permute-done.33
  209.3 6.4 %fusion.11 = f32[16,64,129]{2,1,0:T(8,128)S(1)} fusion(f32[16,66,129]{2,1,0:T(8,128)S(1)} %pad_maximum_fusion.1, f32[16,66,129]{2,1,0:T(8,128)S(1)} %pad_maximum_fusion, f32[16,64,129]{2,1,0:T(8,128)} %constant_dynamic-update-slice_fusion), kind=kLoop, calls=%fused_computation.24 | loop fusion | flops 1188864 | bytes 3170304 | tf_op jit(solution)/shard_map/sub | solution.py:80
  217.0 2.5 %fusion.12 = f32[16,65,128]{2,1,0:T(8,128)S(1)} fusion(f32[16,1,128]{2,1,0:T(1,128)S(1)} %collective-permute-done.28, f32[16,64,128]{2,1,0:T(8,128)S(1)} %copy-done.23, f32[16,1,128]{2,1,0:T(1,128)S(1)} %collective-permute-done.32, f32[16,64,128]{2,1,0:T(8,128)S(1)} %copy-done.25, f32[16,66,129]{2,1,0:T(8,128)S(1)} %pad_maximum_fusion, ...), kind=kLoop, calls=%fused_computation.35 | loop fusion | flops 1464320 | bytes 3194880 | tf_op jit(solution)/shard_map/sub | solution.py:80
  220.8 3.7 %all-to-all-start = ((f32[16,64,128]{2,0,1:T(8,128)}), f32[16,64,128]{2,0,1:T(8,128)S(1)}, u32[]{:S(2)}, u32[]{:S(2)}) async-start(f32[16,64,128]{2,0,1:T(8,128)} %copy.43), calls=%async_computation | async-start | bytes 1048576 | tf_op jit(solution)/shard_map/all_to_all | solution.py:164
  225.5 8.8 %all-gather = f32[64,64,1]{1,2,0:T(1,128)S(1)} all-gather(f32[16,64,1]{1,2,0:T(1,128)S(1)} %copy.45), channel_id=2, replica_groups=mesh['gx'=4,'gy'=4,'gz'=2] {'gy'}, dimensions={0}, use_global_device_ids=true | all-gather | bytes 20480 | tf_op jit(solution)/shard_map/all_gather | solution.py:34
  235.9 3.5 %all-to-all-start.1 = ((f32[16,64,128]{2,0,1:T(8,128)}), f32[16,64,128]{2,0,1:T(8,128)S(1)}, u32[]{:S(2)}, u32[]{:S(2)}) async-start(f32[16,64,128]{2,0,1:T(8,128)} %copy.46), calls=%async_computation.1 | async-start | bytes 1048576 | tf_op jit(solution)/shard_map/all_to_all | solution.py:165
  240.7 7.4 %all-to-all-done.1 = f32[16,64,128]{2,0,1:T(8,128)S(1)} async-done(((f32[16,64,128]{2,0,1:T(8,128)}), f32[16,64,128]{2,0,1:T(8,128)S(1)}, u32[]{:S(2)}, u32[]{:S(2)}) %all-to-all-start.1) | async-done | bytes 524320 | tf_op jit(solution)/shard_map/all_to_all | solution.py:165
  (193 shorter events, 74.3 us)
Async XLA Ops:
  2.0 19.8 %collective-permute-start.14 = (f32[16,64,1]{2,1,0:T(8,128)S(1)}, f32[16,64,1]{2,1,0:T(8,128)S(1)}, u32[]{:S(2)}, u32[]{:S(2)}) collective-permute-start(f32[16,64,1]{2,1,0:T(8,128)S(1)} %slice.366), channel_id=1, source_target_pairs={{0,2},{2,4},{4,6},{1,3},{3,5},{5,7},{8,10},{10,12},{12,14},{9,11},... | collective-permute-start | bytes 12296 | tf_op jit(solution)/shard_map/ppermute | solution.py:16
  5.3 42.3 %collective-permute-start.13 = (f32[16,1,128]{2,1,0:T(1,128)S(1)}, f32[16,1,128]{2,1,0:T(1,128)S(1)}, u32[]{:S(2)}, u32[]{:S(2)}) collective-permute-start(f32[16,1,128]{2,1,0:T(1,128)S(1)} %slice.357), channel_id=1, source_target_pairs={{0,8},{8,16},{16,24},{1,9},{9,17},{17,25},{2,10},{10,18},{18,26},{... | collective-permute-start | bytes 24584 | tf_op jit(solution)/shard_map/ppermute | solution.py:16
  11.0 67.5 %collective-permute-start = (f32[1,64,128]{2,1,0:T(8,128)}, f32[1,64,128]{2,1,0:T(8,128)S(1)}, u32[]{:S(2)}, u32[]{:S(2)}) collective-permute-start(f32[1,64,128]{2,1,0:T(8,128)} %slice.336), channel_id=1, source_target_pairs={{0,1},{2,3},{4,5},{6,7},{8,9},{10,11},{12,13},{14,15},{16,17},{18,... | collective-permute-start | bytes 98312 | tf_op jit(solution)/shard_map/ppermute | solution.py:16
  15.3 19.1 %collective-permute-start.2 = (f32[16,1,128]{2,1,0:T(1,128)S(1)}, f32[16,1,128]{2,1,0:T(1,128)S(1)}, u32[]{:S(2)}, u32[]{:S(2)}) collective-permute-start(f32[16,1,128]{2,1,0:T(1,128)S(1)} %get-tuple-element.140), channel_id=1, source_target_pairs={{8,0},{16,8},{24,16},{9,1},{17,9},{25,17},{10,2},{18,10},{26,18},{... | collective-permute-start | bytes 24584 | tf_op jit(solution)/shard_map/ppermute | solution.py:27
  17.5 24.7 %collective-permute-start.7 = (f32[16,1,128]{2,1,0:T(1,128)S(1)}, f32[16,1,128]{2,1,0:T(1,128)S(1)}, u32[]{:S(2)}, u32[]{:S(2)}) collective-permute-start(f32[16,1,128]{2,1,0:T(1,128)S(1)} %get-tuple-element.138), channel_id=1, source_target_pairs={{8,0},{16,8},{24,16},{9,1},{17,9},{25,17},{10,2},{18,10},{26,18},{... | collective-permute-start | bytes 24584 | tf_op jit(solution)/shard_map/ppermute | solution.py:27
  22.6 15.7 %collective-permute-start.1 = (f32[16,1,128]{2,1,0:T(1,128)S(1)}, f32[16,1,128]{2,1,0:T(1,128)S(1)}, u32[]{:S(2)}, u32[]{:S(2)}) collective-permute-start(f32[16,1,128]{2,1,0:T(1,128)S(1)} %get-tuple-element.139), channel_id=1, source_target_pairs={{0,8},{8,16},{16,24},{1,9},{9,17},{17,25},{2,10},{10,18},{18,26},{... | collective-permute-start | bytes 24584 | tf_op jit(solution)/shard_map/ppermute | solution.py:26
  34.3 9.1 %collective-permute-start.6 = (f32[16,1,128]{2,1,0:T(1,128)S(1)}, f32[16,1,128]{2,1,0:T(1,128)S(1)}, u32[]{:S(2)}, u32[]{:S(2)}) collective-permute-start(f32[16,1,128]{2,1,0:T(1,128)S(1)} %get-tuple-element.137), channel_id=1, source_target_pairs={{0,8},{8,16},{16,24},{1,9},{9,17},{17,25},{2,10},{10,18},{18,26},{... | collective-permute-start | bytes 24584 | tf_op jit(solution)/shard_map/ppermute | solution.py:26
  38.3 121.3 %collective-permute-start.34 = (f32[16,1,128]{2,1,0:T(1,128)}, f32[16,1,128]{2,1,0:T(1,128)}, u32[]{:S(2)}, u32[]{:S(2)}) collective-permute-start(f32[16,1,128]{2,1,0:T(1,128)} %slice.411), channel_id=1, source_target_pairs={{8,0},{16,8},{24,16},{9,1},{17,9},{25,17},{10,2},{18,10},{26,18},{... | collective-permute-start | bytes 24584 | tf_op jit(solution)/shard_map/ppermute | solution.py:16
  42.2 17.7 %collective-permute-start.4 = (f32[16,66,1]{1,0,2:T(8,128)S(1)}, f32[16,66,1]{1,0,2:T(8,128)S(1)}, u32[]{:S(2)}, u32[]{:S(2)}) collective-permute-start(f32[16,66,1]{1,0,2:T(8,128)S(1)} %copy.16), channel_id=1, source_target_pairs={{2,0},{4,2},{6,4},{3,1},{5,3},{7,5},{10,8},{12,10},{14,12},{11,9},... | collective-permute-start | bytes 12680 | tf_op jit(solution)/shard_map/ppermute | solution.py:27
  46.0 21.8 %collective-permute-start.9 = (f32[16,66,1]{1,0,2:T(8,128)S(1)}, f32[16,66,1]{1,0,2:T(8,128)}, u32[]{:S(2)}, u32[]{:S(2)}) collective-permute-start(f32[16,66,1]{1,0,2:T(8,128)S(1)} %copy.20), channel_id=1, source_target_pairs={{2,0},{4,2},{6,4},{3,1},{5,3},{7,5},{10,8},{12,10},{14,12},{11,9},... | collective-permute-start | bytes 12680 | tf_op jit(solution)/shard_map/ppermute | solution.py:27
  47.6 16.8 %collective-permute-start.3 = (f32[16,66,1]{1,0,2:T(8,128)S(1)}, f32[16,66,1]{1,0,2:T(8,128)S(1)}, u32[]{:S(2)}, u32[]{:S(2)}) collective-permute-start(f32[16,66,1]{1,0,2:T(8,128)S(1)} %copy.15), channel_id=1, source_target_pairs={{0,2},{2,4},{4,6},{1,3},{3,5},{5,7},{8,10},{10,12},{12,14},{9,11},... | collective-permute-start | bytes 12680 | tf_op jit(solution)/shard_map/ppermute | solution.py:26
  59.9 9.8 %collective-permute-start.8 = (f32[16,66,1]{1,0,2:T(8,128)S(1)}, f32[16,66,1]{1,0,2:T(8,128)}, u32[]{:S(2)}, u32[]{:S(2)}) collective-permute-start(f32[16,66,1]{1,0,2:T(8,128)S(1)} %copy.19), channel_id=1, source_target_pairs={{0,2},{2,4},{4,6},{1,3},{3,5},{5,7},{8,10},{10,12},{12,14},{9,11},... | collective-permute-start | bytes 12680 | tf_op jit(solution)/shard_map/ppermute | solution.py:26
  66.5 20.1 %collective-permute-start.5 = (f32[1,66,130]{2,1,0:T(8,128)S(1)}, f32[1,66,130]{2,1,0:T(8,128)S(1)}, u32[]{:S(2)}, u32[]{:S(2)}) collective-permute-start(f32[1,66,130]{2,1,0:T(8,128)S(1)} %get-tuple-element.114), channel_id=1, source_target_pairs={{1,0},{3,2},{5,4},{7,6},{9,8},{11,10},{13,12},{15,14},{17,16},{19,... | collective-permute-start | bytes 102968 | tf_op jit(solution)/shard_map/ppermute | solution.py:27
  72.6 15.4 %collective-permute-start.10 = (f32[1,66,130]{2,1,0:T(8,128)S(1)}, f32[1,66,130]{2,1,0:T(8,128)S(1)}, u32[]{:S(2)}, u32[]{:S(2)}) collective-permute-start(f32[1,66,130]{2,1,0:T(8,128)S(1)} %get-tuple-element.112), channel_id=1, source_target_pairs={{1,0},{3,2},{5,4},{7,6},{9,8},{11,10},{13,12},{15,14},{17,16},{19,... | collective-permute-start | bytes 102968 | tf_op jit(solution)/shard_map/ppermute | solution.py:27
  73.9 14.1 %collective-permute-start.11 = (f32[1,66,130]{2,1,0:T(8,128)S(1)}, f32[1,66,130]{2,1,0:T(8,128)S(1)}, u32[]{:S(2)}, u32[]{:S(2)}) collective-permute-start(f32[1,66,130]{2,1,0:T(8,128)S(1)} %get-tuple-element.113), channel_id=1, source_target_pairs={{0,1},{2,3},{4,5},{6,7},{8,9},{10,11},{12,13},{14,15},{16,17},{18,... | collective-permute-start | bytes 102968 | tf_op jit(solution)/shard_map/ppermute | solution.py:26
  78.5 9.5 %collective-permute-start.12 = (f32[1,66,130]{2,1,0:T(8,128)S(1)}, f32[1,66,130]{2,1,0:T(8,128)S(1)}, u32[]{:S(2)}, u32[]{:S(2)}) collective-permute-start(f32[1,66,130]{2,1,0:T(8,128)S(1)} %get-tuple-element.111), channel_id=1, source_target_pairs={{0,1},{2,3},{4,5},{6,7},{8,9},{10,11},{12,13},{14,15},{16,17},{18,... | collective-permute-start | bytes 102968 | tf_op jit(solution)/shard_map/ppermute | solution.py:26
  86.6 69.6 %collective-permute-start.30 = (f32[16,64,1]{2,1,0:T(8,128)}, f32[16,64,1]{2,1,0:T(8,128)}, u32[]{:S(2)}, u32[]{:S(2)}) collective-permute-start(f32[16,64,1]{2,1,0:T(8,128)} %bitcast.25), channel_id=1, source_target_pairs={{2,0},{4,2},{6,4},{3,1},{5,3},{7,5},{10,8},{12,10},{14,12},{11,9},... | collective-permute-start | bytes 12296 | tf_op jit(solution)/shard_map/ppermute | solution.py:16
  100.3 18.6 %collective-permute-start.16 = (f32[16,1,128]{2,1,0:T(1,128)S(1)}, f32[16,1,128]{2,1,0:T(1,128)S(1)}, u32[]{:S(2)}, u32[]{:S(2)}) collective-permute-start(f32[16,1,128]{2,1,0:T(1,128)S(1)} %get-tuple-element.136), channel_id=1, source_target_pairs={{8,0},{16,8},{24,16},{9,1},{17,9},{25,17},{10,2},{18,10},{26,18},{... | collective-permute-start | bytes 24584 | tf_op jit(solution)/shard_map/ppermute | solution.py:27
  101.6 21.9 %collective-permute-start.15 = (f32[16,1,128]{2,1,0:T(1,128)S(1)}, f32[16,1,128]{2,1,0:T(1,128)S(1)}, u32[]{:S(2)}, u32[]{:S(2)}) collective-permute-start(f32[16,1,128]{2,1,0:T(1,128)S(1)} %get-tuple-element.135), channel_id=1, source_target_pairs={{0,8},{8,16},{16,24},{1,9},{9,17},{17,25},{2,10},{10,18},{18,26},{... | collective-permute-start | bytes 24584 | tf_op jit(solution)/shard_map/ppermute | solution.py:26
  117.6 11.1 %collective-permute-start.21 = (f32[16,1,128]{2,1,0:T(1,128)S(1)}, f32[16,1,128]{2,1,0:T(1,128)S(1)}, u32[]{:S(2)}, u32[]{:S(2)}) collective-permute-start(f32[16,1,128]{2,1,0:T(1,128)S(1)} %get-tuple-element.134), channel_id=1, source_target_pairs={{8,0},{16,8},{24,16},{9,1},{17,9},{25,17},{10,2},{18,10},{26,18},{... | collective-permute-start | bytes 24584 | tf_op jit(solution)/shard_map/ppermute | solution.py:27
  118.9 12.9 %collective-permute-start.20 = (f32[16,1,128]{2,1,0:T(1,128)S(1)}, f32[16,1,128]{2,1,0:T(1,128)S(1)}, u32[]{:S(2)}, u32[]{:S(2)}) collective-permute-start(f32[16,1,128]{2,1,0:T(1,128)S(1)} %get-tuple-element.133), channel_id=1, source_target_pairs={{0,8},{8,16},{16,24},{1,9},{9,17},{17,25},{2,10},{10,18},{18,26},{... | collective-permute-start | bytes 24584 | tf_op jit(solution)/shard_map/ppermute | solution.py:26
  126.1 11.1 %collective-permute-start.18 = (f32[16,66,1]{1,0,2:T(8,128)S(1)}, f32[16,66,1]{1,0,2:T(8,128)S(1)}, u32[]{:S(2)}, u32[]{:S(2)}) collective-permute-start(f32[16,66,1]{1,0,2:T(8,128)S(1)} %copy.28), channel_id=1, source_target_pairs={{2,0},{4,2},{6,4},{3,1},{5,3},{7,5},{10,8},{12,10},{14,12},{11,9},... | collective-permute-start | bytes 12680 | tf_op jit(solution)/shard_map/ppermute | solution.py:27
  128.8 13.7 %collective-permute-start.17 = (f32[16,66,1]{1,0,2:T(8,128)S(1)}, f32[16,66,1]{1,0,2:T(8,128)S(1)}, u32[]{:S(2)}, u32[]{:S(2)}) collective-permute-start(f32[16,66,1]{1,0,2:T(8,128)S(1)} %copy.27), channel_id=1, source_target_pairs={{0,2},{2,4},{4,6},{1,3},{3,5},{5,7},{8,10},{10,12},{12,14},{9,11},... | collective-permute-start | bytes 12680 | tf_op jit(solution)/shard_map/ppermute | solution.py:26
  134.5 12.1 %collective-permute-start.23 = (f32[16,66,1]{1,0,2:T(8,128)S(1)}, f32[16,66,1]{1,0,2:T(8,128)S(1)}, u32[]{:S(2)}, u32[]{:S(2)}) collective-permute-start(f32[16,66,1]{1,0,2:T(8,128)S(1)} %copy.32), channel_id=1, source_target_pairs={{2,0},{4,2},{6,4},{3,1},{5,3},{7,5},{10,8},{12,10},{14,12},{11,9},... | collective-permute-start | bytes 12680 | tf_op jit(solution)/shard_map/ppermute | solution.py:27
  137.2 10.5 %collective-permute-start.22 = (f32[16,66,1]{1,0,2:T(8,128)S(1)}, f32[16,66,1]{1,0,2:T(8,128)S(1)}, u32[]{:S(2)}, u32[]{:S(2)}) collective-permute-start(f32[16,66,1]{1,0,2:T(8,128)S(1)} %copy.31), channel_id=1, source_target_pairs={{0,2},{2,4},{4,6},{1,3},{3,5},{5,7},{8,10},{10,12},{12,14},{9,11},... | collective-permute-start | bytes 12680 | tf_op jit(solution)/shard_map/ppermute | solution.py:26
  145.2 15.9 %collective-permute-start.19 = (f32[1,66,130]{2,1,0:T(8,128)}, f32[1,66,130]{2,1,0:T(8,128)S(1)}, u32[]{:S(2)}, u32[]{:S(2)}) collective-permute-start(f32[1,66,130]{2,1,0:T(8,128)} %get-tuple-element.110), channel_id=1, source_target_pairs={{1,0},{3,2},{5,4},{7,6},{9,8},{11,10},{13,12},{15,14},{17,16},{19,... | collective-permute-start | bytes 102968 | tf_op jit(solution)/shard_map/ppermute | solution.py:27
  150.4 10.7 %collective-permute-start.24 = (f32[1,66,130]{2,1,0:T(8,128)}, f32[1,66,130]{2,1,0:T(8,128)S(1)}, u32[]{:S(2)}, u32[]{:S(2)}) collective-permute-start(f32[1,66,130]{2,1,0:T(8,128)} %get-tuple-element.108), channel_id=1, source_target_pairs={{1,0},{3,2},{5,4},{7,6},{9,8},{11,10},{13,12},{15,14},{17,16},{19,... | collective-permute-start | bytes 102968 | tf_op jit(solution)/shard_map/ppermute | solution.py:27
  151.7 9.4 %collective-permute-start.25 = (f32[1,66,130]{2,1,0:T(8,128)}, f32[1,66,130]{2,1,0:T(8,128)S(1)}, u32[]{:S(2)}, u32[]{:S(2)}) collective-permute-start(f32[1,66,130]{2,1,0:T(8,128)} %get-tuple-element.109), channel_id=1, source_target_pairs={{0,1},{2,3},{4,5},{6,7},{8,9},{10,11},{12,13},{14,15},{16,17},{18,... | collective-permute-start | bytes 102968 | tf_op jit(solution)/shard_map/ppermute | solution.py:26
  178.5 21.6 %collective-permute-start.28 = (f32[16,1,128]{2,1,0:T(1,128)S(1)}, f32[16,1,128]{2,1,0:T(1,128)S(1)}, u32[]{:S(2)}, u32[]{:S(2)}) collective-permute-start(f32[16,1,128]{2,1,0:T(1,128)S(1)} %get-tuple-element.132), channel_id=1, source_target_pairs={{8,0},{16,8},{24,16},{9,1},{17,9},{25,17},{10,2},{18,10},{26,18},{... | collective-permute-start | bytes 24584 | tf_op jit(solution)/shard_map/ppermute | solution.py:27
  179.8 20.3 %collective-permute-start.27 = (f32[16,1,128]{2,1,0:T(1,128)S(1)}, f32[16,1,128]{2,1,0:T(1,128)S(1)}, u32[]{:S(2)}, u32[]{:S(2)}) collective-permute-start(f32[16,1,128]{2,1,0:T(1,128)S(1)} %get-tuple-element.131), channel_id=1, source_target_pairs={{0,8},{8,16},{16,24},{1,9},{9,17},{17,25},{2,10},{10,18},{18,26},{... | collective-permute-start | bytes 24584 | tf_op jit(solution)/shard_map/ppermute | solution.py:26
  220.8 15.0 %all-to-all-start = ((f32[16,64,128]{2,0,1:T(8,128)}), f32[16,64,128]{2,0,1:T(8,128)S(1)}, u32[]{:S(2)}, u32[]{:S(2)}) async-start(f32[16,64,128]{2,0,1:T(8,128)} %copy.43), calls=%async_computation | async-start | bytes 1048576 | tf_op jit(solution)/shard_map/all_to_all | solution.py:164
  235.9 12.3 %all-to-all-start.1 = ((f32[16,64,128]{2,0,1:T(8,128)}), f32[16,64,128]{2,0,1:T(8,128)S(1)}, u32[]{:S(2)}, u32[]{:S(2)}) async-start(f32[16,64,128]{2,0,1:T(8,128)} %copy.46), calls=%async_computation.1 | async-start | bytes 1048576 | tf_op jit(solution)/shard_map/all_to_all | solution.py:165
  (41 other events, 601.7 us)
where the time goes:
time: 253 us; the launch traced here: 249 us
  starting transfers between devices  96 us (38%)
  other arithmetic  89.3 us (35%)
  local copies, waits for them, and re-layouts  42.8 us (17%)
  waiting for transfers between devices  9.47 us (4%)
  blocking collectives  8.85 us (3%)
    ppermute x14, starting transfers between devices, extended(): before = lax.ppermute(last, axis, up)  55.3 us
    add x2, other arithmetic, advance(): centre_real + time_step * ((epsilon - density) * centre_real + lap_real)  29.5 us
    cos x3, other arithmetic, shards(): cosines = [jnp.cos(phase) for phase in link_halo]  21.1 us
    ppermute x16, starting transfers between devices, extended(): after = lax.ppermute(initial, axis, down)  20.9 us
    add x2, other arithmetic, advance(): centre_imag + time_step * ((epsilon - density) * centre_imag + lap_imag)  20.5 us
    ppermute x5, starting transfers between devices, passed_along(): return lax.ppermute(block, axis, route)  12.7 us
    slice x14, local copies, waits for them, and re-layouts, extended(): last = lax.slice_in_dim(x, length - width, length, axis=dim)  9.82 us
    sub x2, other arithmetic, current(): return first_real * turned_imag - first_imag * turned_real  8.93 us
  transfers between devices with their start and end apart: 37, of which 2 were waited for; matrix products, arithmetic and copies ran while one was open for 39% of the time, Pallas kernels for 0%

commit v1 on v0

v1 whole, which is shorter than its diff:
```python
import functools
import math

import jax
import jax.numpy as jnp
from jax import lax
from jax.experimental import pallas as pl
from jax.experimental.pallas import tpu as pltpu
from jax.sharding import PartitionSpec as P

STEPS = 2
LEVELS = 8
DT = 0.15
W = 128
MESH = pl.DeviceIdType.MESH

S = [(-1.0) ** k / (math.factorial(2 * k + 1) * 2.0 ** (2 * k + 1)) for k in range(7)]
C = [(-1.0) ** k / (math.factorial(2 * k) * 2.0 ** (2 * k)) for k in range(7)]


def poly(t, coefs):
    acc = jnp.float32(coefs[-1]) * t + jnp.float32(coefs[-2])
    for c in coefs[-3::-1]:
        acc = acc * t + jnp.float32(c)
    return acc


def cos_sin(x):
    t = x * x
    s = x * poly(t, S)
    c = poly(t, C)
    u = s + s
    return 1.0 - u * s, u * c


def iota(shape, dim):
    return lax.broadcasted_iota(jnp.int32, shape, dim)


def pack_cols(layers, col, nx):
    lane = iota((nx, W), 1)
    acc = jnp.zeros((nx, W), jnp.float32)
    for z, layer in enumerate(layers):
        shift = (z - col) % W
        moved = layer() if shift == 0 else pltpu.roll(layer(), shift, 1)
        acc = jnp.where(lane == z, moved, acc)
    return acc


def kernel(dims, o_r, o_i, p_z, p_x, p_y, mat, lev, fr, fi, circ, flux,
           cs, eps, st, zu_s, zd_s, xu_s, xd_s, yu_s, yd_s,
           zu_r, zd_r, xu_r, xd_r, yu_r, yd_r, ecx, ecy, ecz,
           jj, rj, e_s, e_r, snd, rcv, jsnd, jrcv, esnd, ercv):
    NZ, NX, R, GX, GY, GZ = dims
    gx, gy, gz = (lax.axis_index(a) for a in ("gx", "gy", "gz"))
    lane = iota((NX, W), 1)
    row = iota((NX, W), 0)
    G = GY

    here = {"gx": gx, "gy": gy, "gz": gz}

    def at_device(**other):
        return tuple({**here, **other}[a] for a in ("gx", "gy", "gz"))

    barrier = pltpu.get_barrier_semaphore()

    def greet(cond, who):
        @pl.when(cond)
        def _():
            pl.semaphore_signal(barrier, inc=1, device_id=who, device_id_type=MESH)

    peers = []
    for k in range(1, G):
        peers.append((gx >= 0, at_device(gy=lax.rem(gy + k, G))))
    peers.append((gx > 0, at_device(gx=jnp.maximum(gx - 1, 0))))
    peers.append((gx < GX - 1, at_device(gx=jnp.minimum(gx + 1, GX - 1))))
    peers.append((gz > 0, at_device(gz=jnp.maximum(gz - 1, 0))))
    peers.append((gz < GZ - 1, at_device(gz=jnp.minimum(gz + 1, GZ - 1))))
    peers.append(((gx > 0) & (gy < G - 1), at_device(gx=jnp.maximum(gx - 1, 0), gy=G - 1)))
    for s in range(G - 1):
        peers.append(((gx < GX - 1) & (gy == G - 1), at_device(gx=jnp.minimum(gx + 1, GX - 1), gy=s)))
    for cond, who in peers:
        greet(cond, who)

    up = {
        "z": (gz < GZ - 1, at_device(gz=jnp.minimum(gz + 1, GZ - 1)), gz > 0),
        "x": (gx < GX - 1, at_device(gx=jnp.minimum(gx + 1, GX - 1)), gx > 0),
        "y": (gy < G - 1, at_device(gy=jnp.minimum(gy + 1, G - 1)), gy > 0),
    }
    down = {
        "z": (gz > 0, at_device(gz=jnp.maximum(gz - 1, 0)), gz < GZ - 1),
        "x": (gx > 0, at_device(gx=jnp.maximum(gx - 1, 0)), gx < GX - 1),
        "y": (gy > 0, at_device(gy=jnp.maximum(gy - 1, 0)), gy < G - 1),
    }

    def messages(t):
        out = []
        full = [(yu_s, yu_r, up["y"]), (yd_s, yd_r, down["y"]), (xu_s, xu_r, up["x"]),
                (xd_s, xd_r, down["x"]), (zu_s, zu_r, up["z"]), (zd_s, zd_r, down["z"])]
        for m, (src, dst, (scond, who, rcond)) in enumerate(full):
            if t == STEPS and m not in (1, 3):
                continue
            copy = pltpu.make_async_remote_copy(
                src_ref=src.at[t], dst_ref=dst.at[t], send_sem=snd.at[t * 6 + m],
                recv_sem=rcv.at[t * 6 + m], device_id=who, device_id_type=MESH)
            out.append((copy, scond, rcond, dst.at[t]))
        return out

    rounds = [messages(t) for t in range(STEPS + 1)]

    for msgs in rounds:
        for _, _, rcond, dst in msgs:
            @pl.when(jnp.logical_not(rcond))
            def _(dst=dst):
                dst[...] = jnp.zeros_like(dst)

    def launch(t):
        for copy, scond, _, _ in rounds[t]:
            pl.when(scond)(copy.start)

    def arrive(t):
        for copy, _, rcond, _ in rounds[t]:
            pl.when(rcond)(copy.wait_recv)

    def edges(t, sr, si):
        first_r = pack_cols([lambda z=z: sr[z] for z in range(NZ)], 0, NX)
        first_i = pack_cols([lambda z=z: si[z] for z in range(NZ)], 0, NX)
        yd_s[t] = jnp.where(lane < NZ, first_r, pltpu.roll(first_i, NZ, 1))
        xd_s[t, 0] = sr[:, 0, :]
        xd_s[t, 1] = si[:, 0, :]
        if t == STEPS:
            return
        last_r = pack_cols([lambda z=z: sr[z] for z in range(NZ)], W - 1, NX)
        last_i = pack_cols([lambda z=z: si[z] for z in range(NZ)], W - 1, NX)
        c, s = ecy[0], ecy[1]
        qr, qi = c * last_r + s * last_i, c * last_i - s * last_r
        yu_s[t] = jnp.where(lane < NZ, qr, pltpu.roll(qi, NZ, 1))
        lr, li = sr[:, NX - 1, :], si[:, NX - 1, :]
        c, s = ecx[0], ecx[1]
        xu_s[t, 0] = c * lr + s * li
        xu_s[t, 1] = c * li - s * lr
        zd_s[t, 0] = sr[0]
        zd_s[t, 1] = si[0]
        c, s = ecz[0], ecz[1]
        lr, li = sr[NZ - 1], si[NZ - 1]
        zu_s[t, 0] = c * lr + s * li
        zu_s[t, 1] = c * li - s * lr

    ecx[0], ecx[1] = cos_sin(p_x[:, NX - 1, :])
    ecy[0], ecy[1] = cos_sin(pack_cols([lambda z=z: p_y[z] for z in range(NZ)], W - 1, NX))
    ecz[0], ecz[1] = cos_sin(p_z[NZ - 1])
    edges(0, o_r, o_i)
    count = jnp.int32(0)
    for cond, _ in peers:
        count = count + jnp.where(cond, 1, 0)
    pl.semaphore_wait(barrier, count)
    launch(0)

    def prepare(z, _):
        for m, ref in enumerate((p_z, p_x, p_y)):
            c, s = cos_sin(ref[z])
            cs[2 * m, z] = c
            cs[2 * m + 1, z] = s
        m = mat[z]
        b0, b1, b2 = (m & 1) != 0, (m & 2) != 0, (m & 4) != 0
        quarter = [jnp.where(b0, lev[2 * j + 1], lev[2 * j]) for j in range(4)]
        half = [jnp.where(b1, quarter[2 * j + 1], quarter[2 * j]) for j in range(2)]
        eps[z] = jnp.where(b2, half[1], half[0])
        return 0

    lax.fori_loop(0, NZ, prepare, 0)

    def ahead_x(t, part, z, v):
        halo = xd_r[t, part, pl.ds(z, 1), :]
        return jnp.where(row == NX - 1, halo, pltpu.roll(v, NX - 1, 0))

    def ahead_y(t, part, z, v):
        halo = pltpu.roll(yd_r[t], W - 1 - part * NZ - z, 1)
        return jnp.where(lane == W - 1, halo, pltpu.roll(v, W - 1, 1))

    def step(t, sr, si, dr, di):
        def body(z, carry, az_r, az_i):
            bz_r, bz_i = carry
            r, i = sr[z], si[z]
            lap_r = -6.0 * r + bz_r
            lap_i = -6.0 * i + bz_i
            c, s = cs[0, z], cs[1, z]
            lap_r = lap_r + c * az_r - s * az_i
            lap_i = lap_i + c * az_i + s * az_r
            nz_r, nz_i = c * r + s * i, c * i - s * r
            c, s = cs[2, z], cs[3, z]
            a_r, a_i = ahead_x(t, 0, z, r), ahead_x(t, 1, z, i)
            lap_r = lap_r + c * a_r - s * a_i
            lap_i = lap_i + c * a_i + s * a_r
            q_r, q_i = c * r + s * i, c * i - s * r
            lap_r = lap_r + jnp.where(row == 0, xu_r[t, 0, pl.ds(z, 1), :], pltpu.roll(q_r, 1, 0))
            lap_i = lap_i + jnp.where(row == 0, xu_r[t, 1, pl.ds(z, 1), :], pltpu.roll(q_i, 1, 0))
            c, s = cs[4, z], cs[5, z]
            a_r, a_i = ahead_y(t, 0, z, r), ahead_y(t, 1, z, i)
            lap_r = lap_r + c * a_r - s * a_i
            lap_i = lap_i + c * a_i + s * a_r
            q_r, q_i = c * r + s * i, c * i - s * r
            h_r = pltpu.roll(yu_r[t], (W - z) % W, 1)
            h_i = pltpu.roll(yu_r[t], W - NZ - z, 1)
            lap_r = lap_r + jnp.where(lane == 0, h_r, pltpu.roll(q_r, 1, 1))
            lap_i = lap_i + jnp.where(lane == 0, h_i, pltpu.roll(q_i, 1, 1))
            g = eps[z] - (r * r + i * i)
            dr[z] = r + DT * (g * r + lap_r)
            di[z] = i + DT * (g * i + lap_i)
            return nz_r, nz_i

        carry = (zu_r[t, 0], zu_r[t, 1])
        carry = lax.fori_loop(0, NZ - 1, lambda z, c: body(z, c, sr[z + 1], si[z + 1]), carry)
        body(NZ - 1, carry, zd_r[t, 0], zd_r[t, 1])

    s_r, s_i = st.at[0], st.at[1]
    arrive(0)
    step(0, o_r, o_i, s_r, s_i)
    edges(1, s_r, s_i)
    launch(1)
    arrive(1)
    step(1, s_r, s_i, fr, fi)
    edges(2, fr, fi)
    launch(2)
    arrive(2)

    mine = pl.ds(pl.multiple_of(gy * R, R), R)

    def currents(z, _):
        r, i = fr[z], fi[z]
        c, s = cs[2, z], cs[3, z]
        a_r, a_i = ahead_x(2, 0, z, r), ahead_x(2, 1, z, i)
        jj[0, z] = r * (c * a_i + s * a_r) - i * (c * a_r - s * a_i)
        c, s = cs[4, z], cs[5, z]
        a_r, a_i = ahead_y(2, 0, z, r), ahead_y(2, 1, z, i)
        j_y = r * (c * a_i + s * a_r) - i * (c * a_r - s * a_i)
        jj[1, z] = j_y
        for d in range(G):
            at = (R * (d + 1)) % NX
            e_s[d, pl.ds(z, 1), :] = j_y[at:at + 1, :]
        return 0

    lax.fori_loop(0, NZ, currents, 0)

    def slab_copy(k):
        to = lax.rem(gy + k, G)
        rows = pl.ds(pl.multiple_of(to * R, R), R)
        return pltpu.make_async_remote_copy(
            src_ref=jj.at[:, :, rows, :], dst_ref=rj.at[k], send_sem=jsnd.at[k],
            recv_sem=jrcv.at[k], device_id=at_device(gy=to), device_id_type=MESH)

    def row_copy(k):
        to = lax.rem(gy + k, G)
        return pltpu.make_async_remote_copy(
            src_ref=e_s.at[to], dst_ref=e_r.at[k], send_sem=esnd.at[k],
            recv_sem=ercv.at[k], device_id=at_device(gy=to), device_id_type=MESH)

    def last_row_copy(k):
        return pltpu.make_async_remote_copy(
            src_ref=e_s.at[G - 1], dst_ref=e_r.at[k], send_sem=esnd.at[G],
            recv_sem=ercv.at[k], device_id=at_device(gx=jnp.maximum(gx - 1, 0), gy=G - 1),
            device_id_type=MESH)

    slabs = [slab_copy(k) for k in range(1, G)]
    for copy in slabs:
        copy.start()
    for k in range(1, G):
        pl.when(lax.rem(gy + k, G) != G - 1)(row_copy(k).start)
    pl.when(gx > 0)(last_row_copy(G - 1 - gy).start)

    rj[0] = jj[:, :, mine, :]

    @pl.when(gy < G - 1)
    def _():
        e_r[0] = e_s[gy]

    @pl.when((gy == G - 1) & (gx == GX - 1))
    def _():
        e_r[...] = jnp.zeros_like(e_r)

    for copy in slabs:
        copy.wait_recv()

    @pl.when(gy < G - 1)
    def _():
        for k in range(1, G):
            row_copy(k).wait_recv()

    @pl.when((gy == G - 1) & (gx < GX - 1))
    def _():
        for k in range(G):
            last_row_copy(k).wait_recv()

    ZC = 4
    rows_n = ZC * R
    lane_s = iota((rows_n, W), 1)
    row_s = iota((ZC, R, W), 1)

    def slab(b, _):
        zs = pl.ds(b * ZC, ZC)
        slot = [lax.rem(gy - s + G, G) for s in range(G)]
        jx = [rj[slot[s], 0, zs].reshape(rows_n, W) for s in range(G)]
        total = jnp.zeros((rows_n, 1), jnp.float32)
        for s in range(G):
            v = jx[s]
            d = 1
            while d < W:
                v = v + jnp.where(lane_s >= d, pltpu.roll(v, d, 1), 0.0)
                d *= 2
            v = v + total
            total = v[:, W - 1:W]
            flux[zs, :, s * W:(s + 1) * W] = v.reshape(ZC, R, W)
            j_y = rj[slot[s], 1, zs]
            extra = e_r[slot[s], zs, :].reshape(ZC, 1, W)
            j_y_next = jnp.where(row_s == R - 1, extra, pltpu.roll(j_y, R - 1, 1))
            after = jx[s + 1][:, 0:1] if s < G - 1 else jnp.zeros((rows_n, 1), jnp.float32)
            j_x_next = jnp.where(lane_s == W - 1, after, pltpu.roll(jx[s], W - 1, 1))
            circ[zs, :, s * W:(s + 1) * W] = (
                (jx[s] - j_x_next).reshape(ZC, R, W) + j_y_next - j_y)
        return 0

    lax.fori_loop(0, NZ // ZC, slab, 0)

    for msgs in rounds:
        for copy, scond, _, _ in msgs:
            pl.when(scond)(copy.wait_send)
    for copy in slabs:
        copy.wait_send()
    for k in range(1, G):
        pl.when(lax.rem(gy + k, G) != G - 1)(row_copy(k).wait_send)
    pl.when(gx > 0)(last_row_copy(0).wait_send)


def solution(mesh):
    GX, GY, GZ = (mesh.shape[a] for a in ("gx", "gy", "gz"))

    def shards(o_r, o_i, p_z, p_x, p_y, mat, lev):
        NZ, NX, NY = o_r.shape
        assert NY == W and 2 * NZ <= W and NX % (8 * GY) == 0 and NZ % 4 == 0
        R = NX // GY
        f32 = jnp.float32
        T = STEPS + 1
        vm = lambda *shape: pltpu.VMEM(shape, f32)
        vspec = pl.BlockSpec(memory_space=pltpu.VMEM)
        sspec = pl.BlockSpec(memory_space=pltpu.SMEM)
        dma = pltpu.SemaphoreType.DMA
        layers = lambda: [vm(T, 2, NX, W), vm(T, 2, NX, W), vm(T, 2, NZ, W), vm(T, 2, NZ, W),
                          vm(T, NX, W), vm(T, NX, W)]
        return pl.pallas_call(
            functools.partial(kernel, (NZ, NX, R, GX, GY, GZ)),
            out_shape=[jax.ShapeDtypeStruct((NZ, NX, W), f32)] * 2
            + [jax.ShapeDtypeStruct((NZ, R, GY * W), f32)] * 2,
            in_specs=[vspec] * 6 + [sspec],
            out_specs=[vspec] * 4,
            scratch_shapes=[vm(6, NZ, NX, W), vm(NZ, NX, W), vm(2, NZ, NX, W)]
            + layers() + layers()
            + [vm(2, NZ, W), vm(2, NX, W), vm(2, NX, W),
               vm(2, NZ, NX, W), vm(GY, 2, NZ, R, W), vm(GY, NZ, W), vm(GY, NZ, W),
               dma((6 * T,)), dma((6 * T,)), dma((GY,)), dma((GY,)), dma((GY + 1,)), dma((GY,))],
            compiler_params=pltpu.CompilerParams(
                collective_id=0, has_side_effects=True, vmem_limit_bytes=48 * 1024 * 1024),
        )(o_r, o_i, p_z, p_x, p_y, mat, lev)

    block = P("gz", "gx", "gy")
    line = P("gz", ("gx", "gy"), None)
    return jax.shard_map(shards, mesh=mesh, in_specs=(block,) * 6 + (P(),),
                         out_specs=(block, block, line, line), check_vma=False)
```

time: 253 us -> 48.1 us (0.19); the launches traced: 249 us -> 47.7 us
  starting transfers between devices: 96 us -> 0 us
  other arithmetic: 89.3 us -> 0 us
  Pallas kernels: 0 us -> 37 us
  local copies, waits for them, and re-layouts: 42.8 us -> 10.1 us
  waiting for transfers between devices: 9.47 us -> 0 us
  blocking collectives: 8.85 us -> 0 us
    ppermute x35 -> x0, starting transfers between devices: 88.9 us -> none  [the longest x14 55.3 us: extended(): before = lax.ppermute(last, axis, up)]
    add x6 -> x0, other arithmetic: 50.6 us -> none  [the longest x2 29.5 us: advance(): centre_real + time_step * ((epsilon - density) * centre_real + lap_real)]
    pallas_call x0 -> x1, Pallas kernels: none -> 37 us  [shards(): pl.pallas_call(functools.partial(kernel, (NZ, NX, R, GX, GY, GZ)), out_sh...]
    cos x3 -> x0, other arithmetic: 21.1 us -> none  [shards(): cosines = [jnp.cos(phase) for phase in link_halo]]
    slice x27 -> x0, local copies, waits for them, and re-layouts: 20.7 us -> none  [the longest x14 9.82 us: extended(): last = lax.slice_in_dim(x, length - width, length, axis=dim)]
    ppermute x10 -> x0, local copies, waits for them, and re-layouts: 11.1 us -> none  [the longest x6 5.87 us: extended(): after = lax.ppermute(initial, axis, down)]
    sub x4 -> x0, other arithmetic: 9.56 us -> none  [the longest x2 8.93 us: current(): return first_real * turned_imag - first_imag * turned_real]
    all_gather x1 -> x0, blocking collectives: 8.85 us -> none  [prefix(): pieces = lax.all_gather(value, axis)]
  transfers between devices with their start and end apart: 37 -> 0, of which waited for: 2 -> 0; matrix products, arithmetic and copies ran while one was open for 39% -> 0% of each run, Pallas kernels for 0% -> 0%
where the time goes in v1:
time: 48.1 us; the launch traced here: 47.7 us
  Pallas kernels  37 us (77%)
  local copies, waits for them, and re-layouts  10.1 us (21%)
  between operations  0.66 us (1%)
    pallas_call x1, Pallas kernels, shards(): pl.pallas_call(functools.partial(kernel, (NZ, NX, R, GX, GY, GZ)), out_sh...  37 us
    unnamed x18, local copies, waits for them, and re-layouts  10.1 us

profile of v1, /device:TPU:0, one launch (start us, length us, event | category | flops | bytes accessed | tf_op | source)
XLA Modules:
  0.0 47.7 jit_solution(4852143890936608442)
XLA Ops:
  0.6 0.0 copy-start
  0.6 1.0 %copy-done = f32[16,64,128]{2,1,0:T(8,128)S(1)} copy-done((f32[16,64,128]{2,1,0:T(8,128)S(1)}, f32[16,64,128]{2,1,0:T(8,128)}, u32[]{:S(2)}) %copy-start) | copy-done | bytes 524312
  1.7 0.0 copy-start.1
  1.7 1.0 %copy-done.1 = f32[16,64,128]{2,1,0:T(8,128)S(1)} copy-done((f32[16,64,128]{2,1,0:T(8,128)S(1)}, f32[16,64,128]{2,1,0:T(8,128)}, u32[]{:S(2)}) %copy-start.1) | copy-done | bytes 524312
  2.7 0.0 copy-start.2
  2.7 1.0 %copy-done.2 = f32[16,64,128]{2,1,0:T(8,128)S(1)} copy-done((f32[16,64,128]{2,1,0:T(8,128)S(1)}, f32[16,64,128]{2,1,0:T(8,128)}, u32[]{:S(2)}) %copy-start.2) | copy-done | bytes 524312
  3.8 0.0 copy-start.3
  3.8 1.0 %copy-done.3 = f32[16,64,128]{2,1,0:T(8,128)S(1)} copy-done((f32[16,64,128]{2,1,0:T(8,128)S(1)}, f32[16,64,128]{2,1,0:T(8,128)}, u32[]{:S(2)}) %copy-start.3) | copy-done | bytes 524312
  4.8 0.0 copy-start.4
  4.8 1.0 %copy-done.4 = f32[16,64,128]{2,1,0:T(8,128)S(1)} copy-done((f32[16,64,128]{2,1,0:T(8,128)S(1)}, f32[16,64,128]{2,1,0:T(8,128)}, u32[]{:S(2)}) %copy-start.4) | copy-done | bytes 524312
  5.8 0.0 copy-start.5
  5.8 1.0 %copy-done.5 = s32[16,64,128]{2,1,0:T(8,128)S(1)} copy-done((s32[16,64,128]{2,1,0:T(8,128)S(1)}, s32[16,64,128]{2,1,0:T(8,128)}, u32[]{:S(2)}) %copy-start.5) | copy-done | bytes 524312
  6.9 0.0 copy-start.6
  6.9 0.7 %copy-done.6 = f32[8]{0:T(128)S(1)} copy-done((f32[8]{0:T(128)S(1)}, f32[8]{0:T(128)}, u32[]{:S(2)}) %copy-start.6) | copy-done | bytes 56
  7.5 37.0 %shard_map.102 = (f32[16,64,128]{2,1,0:T(8,128)S(1)}, f32[16,64,128]{2,1,0:T(8,128)S(1)}, f32[16,16,512]{2,1,0:T(8,128)S(1)}, f32[16,16,512]{2,1,0:T(8,128)S(1)}) custom-call(f32[16,64,128]{2,1,0:T(8,128)S(1)} %copy-done, f32[16,64,128]{2,1,0:T(8,128)S(1)} %copy-done.1, f32[16,64,128]{2,1,0:T(8,128)S(1)} %copy-done.2, f32[16,64,128]{2,1,0:T(8,128)S(1)} %copy-done.3, ...), custom_call_target="tpu_custom_call" | custom-call | tf_op jit(solution)/shard_map/pallas_call | solution.py:349
  44.5 0.8 %copy.15 = f32[16,64,128]{2,1,0:T(8,128)} copy(f32[16,64,128]{2,1,0:T(8,128)S(1)} %get-tuple-element.8) | data formatting | bytes 1048576
  45.3 0.8 %copy.16 = f32[16,64,128]{2,1,0:T(8,128)} copy(f32[16,64,128]{2,1,0:T(8,128)S(1)} %get-tuple-element.9) | data formatting | bytes 1048576
  46.1 0.8 %copy.17 = f32[16,16,512]{2,1,0:T(8,128)} copy(f32[16,16,512]{2,1,0:T(8,128)S(1)} %get-tuple-element.10) | data formatting | bytes 1048576
  46.9 0.8 %copy.18 = f32[16,16,512]{2,1,0:T(8,128)} copy(f32[16,16,512]{2,1,0:T(8,128)S(1)} %get-tuple-element.11) | data formatting | bytes 1048576
Async XLA Ops:
  0.6 1.0 %copy-start = (f32[16,64,128]{2,1,0:T(8,128)S(1)}, f32[16,64,128]{2,1,0:T(8,128)}, u32[]{:S(2)}) copy-start(f32[16,64,128]{2,1,0:T(8,128)} %o_r.1) | copy-start | bytes 1572868
  1.7 1.0 %copy-start.1 = (f32[16,64,128]{2,1,0:T(8,128)S(1)}, f32[16,64,128]{2,1,0:T(8,128)}, u32[]{:S(2)}) copy-start(f32[16,64,128]{2,1,0:T(8,128)} %o_i.1) | copy-start | bytes 1572868
  2.7 1.0 %copy-start.2 = (f32[16,64,128]{2,1,0:T(8,128)S(1)}, f32[16,64,128]{2,1,0:T(8,128)}, u32[]{:S(2)}) copy-start(f32[16,64,128]{2,1,0:T(8,128)} %p_z.1) | copy-start | bytes 1572868
  3.8 1.0 %copy-start.3 = (f32[16,64,128]{2,1,0:T(8,128)S(1)}, f32[16,64,128]{2,1,0:T(8,128)}, u32[]{:S(2)}) copy-start(f32[16,64,128]{2,1,0:T(8,128)} %p_x.1) | copy-start | bytes 1572868
  4.8 1.0 %copy-start.4 = (f32[16,64,128]{2,1,0:T(8,128)S(1)}, f32[16,64,128]{2,1,0:T(8,128)}, u32[]{:S(2)}) copy-start(f32[16,64,128]{2,1,0:T(8,128)} %p_y.1) | copy-start | bytes 1572868
  5.8 1.0 %copy-start.5 = (s32[16,64,128]{2,1,0:T(8,128)S(1)}, s32[16,64,128]{2,1,0:T(8,128)}, u32[]{:S(2)}) copy-start(s32[16,64,128]{2,1,0:T(8,128)} %mat.1) | copy-start | bytes 1572868
  6.9 0.7 %copy-start.6 = (f32[8]{0:T(128)S(1)}, f32[8]{0:T(128)}, u32[]{:S(2)}) copy-start(f32[8]{0:T(128)} %lev.1) | copy-start | bytes 100

commit v2 on v1

--- a/solution.py
+++ b/solution.py
@@ -12,6 +12,7 @@
 LEVELS = 8
 DT = 0.15
 W = 128
+ZC = 4
 MESH = pl.DeviceIdType.MESH
 
 S = [(-1.0) ** k / (math.factorial(2 * k + 1) * 2.0 ** (2 * k + 1)) for k in range(7)]
@@ -47,15 +48,20 @@
     return acc
 
 
-def kernel(dims, o_r, o_i, p_z, p_x, p_y, mat, lev, fr, fi, circ, flux,
-           cs, eps, st, zu_s, zd_s, xu_s, xd_s, yu_s, yd_s,
+def kernel(dims, h0, h1, h2, h3, h4, h5, lev, fr, fi, circ, flux,
+           o_r, o_i, p_z, p_x, p_y, mat, cs, eps, st, zu_s, zd_s, xu_s, xd_s, yu_s, yd_s,
            zu_r, zd_r, xu_r, xd_r, yu_r, yd_r, ecx, ecy, ecz,
-           jj, rj, e_s, e_r, snd, rcv, jsnd, jrcv, esnd, ercv):
+           jj, rj, e_s, e_r, fx_s, fx_r, fy_s, fy_r,
+           insem, snd, rcv, jsnd, jrcv, esnd, ercv, fsnd, frcv):
     NZ, NX, R, GX, GY, GZ = dims
     gx, gy, gz = (lax.axis_index(a) for a in ("gx", "gy", "gz"))
     lane = iota((NX, W), 1)
     row = iota((NX, W), 0)
     G = GY
+    loads = [pltpu.make_async_copy(h, v, insem.at[n]) for n, (h, v) in enumerate(
+        ((h3, p_x), (h4, p_y), (h0, o_r), (h1, o_i), (h2, p_z), (h5, mat)))]
+    for load in loads:
+        load.start()
 
     here = {"gx": gx, "gy": gy, "gz": gz}
 
@@ -98,28 +104,37 @@
         full = [(yu_s, yu_r, up["y"]), (yd_s, yd_r, down["y"]), (xu_s, xu_r, up["x"]),
                 (xd_s, xd_r, down["x"]), (zu_s, zu_r, up["z"]), (zd_s, zd_r, down["z"])]
         for m, (src, dst, (scond, who, rcond)) in enumerate(full):
-            if t == STEPS and m not in (1, 3):
-                continue
             copy = pltpu.make_async_remote_copy(
                 src_ref=src.at[t], dst_ref=dst.at[t], send_sem=snd.at[t * 6 + m],
                 recv_sem=rcv.at[t * 6 + m], device_id=who, device_id_type=MESH)
             out.append((copy, scond, rcond, dst.at[t]))
         return out
 
-    rounds = [messages(t) for t in range(STEPS + 1)]
-
-    for msgs in rounds:
+    rounds = [messages(t) for t in range(STEPS)]
+    NB = NZ // ZC
+    final = []
+    for b in range(NB):
+        pair = []
+        for m, (src, dst, (scond, who, rcond)) in enumerate(
+                ((fy_s, fy_r, down["y"]), (fx_s, fx_r, down["x"]))):
+            copy = pltpu.make_async_remote_copy(
+                src_ref=src.at[b], dst_ref=dst.at[b], send_sem=fsnd.at[2 * b + m],
+                recv_sem=frcv.at[2 * b + m], device_id=who, device_id_type=MESH)
+            pair.append((copy, scond, rcond, dst.at[b]))
+        final.append(pair)
+
+    for msgs in rounds + final:
         for _, _, rcond, dst in msgs:
             @pl.when(jnp.logical_not(rcond))
             def _(dst=dst):
                 dst[...] = jnp.zeros_like(dst)
 
-    def launch(t):
-        for copy, scond, _, _ in rounds[t]:
+    def launch(msgs):
+        for copy, scond, _, _ in msgs:
             pl.when(scond)(copy.start)
 
-    def arrive(t):
-        for copy, _, rcond, _ in rounds[t]:
+    def arrive(msgs):
+        for copy, _, rcond, _ in msgs:
             pl.when(rcond)(copy.wait_recv)
 
     def edges(t, sr, si):
@@ -128,8 +143,6 @@
         yd_s[t] = jnp.where(lane < NZ, first_r, pltpu.roll(first_i, NZ, 1))
         xd_s[t, 0] = sr[:, 0, :]
         xd_s[t, 1] = si[:, 0, :]
-        if t == STEPS:
-            return
         last_r = pack_cols([lambda z=z: sr[z] for z in range(NZ)], W - 1, NX)
         last_i = pack_cols([lambda z=z: si[z] for z in range(NZ)], W - 1, NX)
         c, s = ecy[0], ecy[1]
@@ -146,6 +159,8 @@
         zu_s[t, 0] = c * lr + s * li
         zu_s[t, 1] = c * li - s * lr
 
+    for load in loads[:5]:
+        load.wait()
     ecx[0], ecx[1] = cos_sin(p_x[:, NX - 1, :])
     ecy[0], ecy[1] = cos_sin(pack_cols([lambda z=z: p_y[z] for z in range(NZ)], W - 1, NX))
     ecz[0], ecz[1] = cos_sin(p_z[NZ - 1])
@@ -154,7 +169,8 @@
     for cond, _ in peers:
         count = count + jnp.where(cond, 1, 0)
     pl.semaphore_wait(barrier, count)
-    launch(0)
+    launch(rounds[0])
+    loads[5].wait()
 
     def prepare(z, _):
         for m, ref in enumerate((p_z, p_x, p_y)):
@@ -209,97 +225,115 @@
             di[z] = i + DT * (g * i + lap_i)
             return nz_r, nz_i
 
-        carry = (zu_r[t, 0], zu_r[t, 1])
-        carry = lax.fori_loop(0, NZ - 1, lambda z, c: body(z, c, sr[z + 1], si[z + 1]), carry)
-        body(NZ - 1, carry, zd_r[t, 0], zd_r[t, 1])
+        def run(start, stop, carry):
+            inner = min(stop, NZ - 1)
+            carry = lax.fori_loop(
+                start, inner, lambda z, c: body(z, c, sr[z + 1], si[z + 1]), carry)
+            if stop == NZ:
+                carry = body(NZ - 1, carry, zd_r[t, 0], zd_r[t, 1])
+            return carry
+
+        return run
 
     s_r, s_i = st.at[0], st.at[1]
-    arrive(0)
-    step(0, o_r, o_i, s_r, s_i)
+    arrive(rounds[0])
+    step(0, o_r, o_i, s_r, s_i)(0, NZ, (zu_r[0, 0], zu_r[0, 1]))
     edges(1, s_r, s_i)
-    launch(1)
-    arrive(1)
-    step(1, s_r, s_i, fr, fi)
-    edges(2, fr, fi)
-    launch(2)
-    arrive(2)
-
+    launch(rounds[1])
     mine = pl.ds(pl.multiple_of(gy * R, R), R)
 
-    def currents(z, _):
-        r, i = fr[z], fi[z]
-        c, s = cs[2, z], cs[3, z]
-        a_r, a_i = ahead_x(2, 0, z, r), ahead_x(2, 1, z, i)
-        jj[0, z] = r * (c * a_i + s * a_r) - i * (c * a_r - s * a_i)
-        c, s = cs[4, z], cs[5, z]
-        a_r, a_i = ahead_y(2, 0, z, r), ahead_y(2, 1, z, i)
-        j_y = r * (c * a_i + s * a_r) - i * (c * a_r - s * a_i)
-        jj[1, z] = j_y
-        for d in range(G):
-            at = (R * (d + 1)) % NX
-            e_s[d, pl.ds(z, 1), :] = j_y[at:at + 1, :]
-        return 0
-
-    lax.fori_loop(0, NZ, currents, 0)
-
-    def slab_copy(k):
+    def slab_copy(b, k):
         to = lax.rem(gy + k, G)
         rows = pl.ds(pl.multiple_of(to * R, R), R)
         return pltpu.make_async_remote_copy(
-            src_ref=jj.at[:, :, rows, :], dst_ref=rj.at[k], send_sem=jsnd.at[k],
-            recv_sem=jrcv.at[k], device_id=at_device(gy=to), device_id_type=MESH)
-
-    def row_copy(k):
+            src_ref=jj.at[b, :, :, rows, :], dst_ref=rj.at[b, k], send_sem=jsnd.at[b * G + k],
+            recv_sem=jrcv.at[b * G + k], device_id=at_device(gy=to), device_id_type=MESH)
+
+    def row_copy(b, k):
         to = lax.rem(gy + k, G)
         return pltpu.make_async_remote_copy(
-            src_ref=e_s.at[to], dst_ref=e_r.at[k], send_sem=esnd.at[k],
-            recv_sem=ercv.at[k], device_id=at_device(gy=to), device_id_type=MESH)
-
-    def last_row_copy(k):
+            src_ref=e_s.at[b, to], dst_ref=e_r.at[b, k], send_sem=esnd.at[b * (G + 1) + k],
+            recv_sem=ercv.at[b * G + k], device_id=at_device(gy=to), device_id_type=MESH)
+
+    def last_row_copy(b, k):
         return pltpu.make_async_remote_copy(
-            src_ref=e_s.at[G - 1], dst_ref=e_r.at[k], send_sem=esnd.at[G],
-            recv_sem=ercv.at[k], device_id=at_device(gx=jnp.maximum(gx - 1, 0), gy=G - 1),
-            device_id_type=MESH)
-
-    slabs = [slab_copy(k) for k in range(1, G)]
-    for copy in slabs:
-        copy.start()
-    for k in range(1, G):
-        pl.when(lax.rem(gy + k, G) != G - 1)(row_copy(k).start)
-    pl.when(gx > 0)(last_row_copy(G - 1 - gy).start)
-
-    rj[0] = jj[:, :, mine, :]
-
-    @pl.when(gy < G - 1)
-    def _():
-        e_r[0] = e_s[gy]
+            src_ref=e_s.at[b, G - 1], dst_ref=e_r.at[b, k], send_sem=esnd.at[b * (G + 1) + G],
+            recv_sem=ercv.at[b * G + k],
+            device_id=at_device(gx=jnp.maximum(gx - 1, 0), gy=G - 1), device_id_type=MESH)
 
     @pl.when((gy == G - 1) & (gx == GX - 1))
     def _():
         e_r[...] = jnp.zeros_like(e_r)
 
-    for copy in slabs:
-        copy.wait_recv()
-
-    @pl.when(gy < G - 1)
-    def _():
+    def faces(b):
+        zs = range(b * ZC, (b + 1) * ZC)
+        first_r = pack_cols([lambda z=z: fr[z] for z in zs], 0, NX)
+        first_i = pack_cols([lambda z=z: fi[z] for z in zs], 0, NX)
+        fy_s[b] = jnp.where(lane < ZC, first_r, pltpu.roll(first_i, ZC, 1))
+        for j, z in enumerate(zs):
+            fx_s[b, j:j + 1, :] = fr[z, 0:1, :]
+            fx_s[b, ZC + j:ZC + j + 1, :] = fi[z, 0:1, :]
+
+    def currents(b):
+        def near_x(part, j, v):
+            halo = fx_r[b, pl.ds(part * ZC + j, 1), :]
+            return jnp.where(row == NX - 1, halo, pltpu.roll(v, NX - 1, 0))
+
+        def near_y(part, j, v):
+            halo = pltpu.roll(fy_r[b], W - 1 - part * ZC - j, 1)
+            return jnp.where(lane == W - 1, halo, pltpu.roll(v, W - 1, 1))
+
+        def body(j, _):
+            z = b * ZC + j
+            r, i = fr[z], fi[z]
+            c, s = cs[2, z], cs[3, z]
+            a_r, a_i = near_x(0, j, r), near_x(1, j, i)
+            jj[b, 0, j] = r * (c * a_i + s * a_r) - i * (c * a_r - s * a_i)
+            c, s = cs[4, z], cs[5, z]
+            a_r, a_i = near_y(0, j, r), near_y(1, j, i)
+            j_y = r * (c * a_i + s * a_r) - i * (c * a_r - s * a_i)
+            jj[b, 1, j] = j_y
+            for d in range(G):
+                at = (R * (d + 1)) % NX
+                e_s[b, d, pl.ds(j, 1), :] = j_y[at:at + 1, :]
+            return 0
+
+        lax.fori_loop(0, ZC, body, 0)
+
+    def send(b):
         for k in range(1, G):
-            row_copy(k).wait_recv()
-
-    @pl.when((gy == G - 1) & (gx < GX - 1))
-    def _():
-        for k in range(G):
-            last_row_copy(k).wait_recv()
-
-    ZC = 4
+            pl.when(lax.rem(gy + k, G) != G - 1)(row_copy(b, k).start)
+        pl.when(gx > 0)(last_row_copy(b, G - 1 - gy).start)
+        for k in range(1, G):
+            slab_copy(b, k).start()
+        rj[b, 0] = jj[b, :, :, mine, :]
+
+        @pl.when(gy < G - 1)
+        def _():
+            e_r[b, 0] = e_s[b, gy]
+
+    def receive(b):
+        for k in range(1, G):
+            slab_copy(b, k).wait_recv()
+
+        @pl.when(gy < G - 1)
+        def _():
+            for k in range(1, G):
+                row_copy(b, k).wait_recv()
+
+        @pl.when((gy == G - 1) & (gx < GX - 1))
+        def _():
+            for k in range(G):
+                last_row_copy(b, k).wait_recv()
+
     rows_n = ZC * R
     lane_s = iota((rows_n, W), 1)
     row_s = iota((ZC, R, W), 1)
-
-    def slab(b, _):
-        zs = pl.ds(b * ZC, ZC)
-        slot = [lax.rem(gy - s + G, G) for s in range(G)]
-        jx = [rj[slot[s], 0, zs].reshape(rows_n, W) for s in range(G)]
+    slot = [lax.rem(gy - s + G, G) for s in range(G)]
+
+    def slab(b):
+        zs = slice(b * ZC, (b + 1) * ZC)
+        jx = [rj[b, slot[s], 0].reshape(rows_n, W) for s in range(G)]
         total = jnp.zeros((rows_n, 1), jnp.float32)
         for s in range(G):
             v = jx[s]
@@ -310,25 +344,38 @@
             v = v + total
             total = v[:, W - 1:W]
             flux[zs, :, s * W:(s + 1) * W] = v.reshape(ZC, R, W)
-            j_y = rj[slot[s], 1, zs]
-            extra = e_r[slot[s], zs, :].reshape(ZC, 1, W)
+            j_y = rj[b, slot[s], 1]
+            extra = e_r[b, slot[s]].reshape(ZC, 1, W)
             j_y_next = jnp.where(row_s == R - 1, extra, pltpu.roll(j_y, R - 1, 1))
             after = jx[s + 1][:, 0:1] if s < G - 1 else jnp.zeros((rows_n, 1), jnp.float32)
             j_x_next = jnp.where(lane_s == W - 1, after, pltpu.roll(jx[s], W - 1, 1))
             circ[zs, :, s * W:(s + 1) * W] = (
                 (jx[s] - j_x_next).reshape(ZC, R, W) + j_y_next - j_y)
-        return 0
-
-    lax.fori_loop(0, NZ // ZC, slab, 0)
-
-    for msgs in rounds:
+
+    arrive(rounds[1])
+    second = step(1, s_r, s_i, fr, fi)
+    carry = (zu_r[1, 0], zu_r[1, 1])
+    for b in range(NB + 1):
+        if b < NB:
+            carry = second(b * ZC, (b + 1) * ZC, carry)
+            faces(b)
+            launch(final[b])
+        if b > 0:
+            arrive(final[b - 1])
+            currents(b - 1)
+            send(b - 1)
+    for b in range(NB):
+        receive(b)
+        slab(b)
+
+    for msgs in rounds + final:
         for copy, scond, _, _ in msgs:
             pl.when(scond)(copy.wait_send)
-    for copy in slabs:
-        copy.wait_send()
-    for k in range(1, G):
-        pl.when(lax.rem(gy + k, G) != G - 1)(row_copy(k).wait_send)
-    pl.when(gx > 0)(last_row_copy(0).wait_send)
+    for b in range(NB):
+        for k in range(1, G):
+            slab_copy(b, k).wait_send()
+            pl.when(lax.rem(gy + k, G) != G - 1)(row_copy(b, k).wait_send)
+        pl.when(gx > 0)(last_row_copy(b, 0).wait_send)
 
 
 def solution(mesh):
@@ -336,12 +383,14 @@
 
     def shards(o_r, o_i, p_z, p_x, p_y, mat, lev):
         NZ, NX, NY = o_r.shape
-        assert NY == W and 2 * NZ <= W and NX % (8 * GY) == 0 and NZ % 4 == 0
+        assert NY == W and 2 * NZ <= W and NX % (8 * GY) == 0 and NZ % ZC == 0
         R = NX // GY
         f32 = jnp.float32
-        T = STEPS + 1
+        T = STEPS
+        NB = NZ // ZC
         vm = lambda *shape: pltpu.VMEM(shape, f32)
         vspec = pl.BlockSpec(memory_space=pltpu.VMEM)
+        hspec = pl.BlockSpec(memory_space=pl.ANY)
         sspec = pl.BlockSpec(memory_space=pltpu.SMEM)
         dma = pltpu.SemaphoreType.DMA
         layers = lambda: [vm(T, 2, NX, W), vm(T, 2, NX, W), vm(T, 2, NZ, W), vm(T, 2, NZ, W),
@@ -350,15 +399,18 @@
             functools.partial(kernel, (NZ, NX, R, GX, GY, GZ)),
             out_shape=[jax.ShapeDtypeStruct((NZ, NX, W), f32)] * 2
             + [jax.ShapeDtypeStruct((NZ, R, GY * W), f32)] * 2,
-            in_specs=[vspec] * 6 + [sspec],
+            in_specs=[hspec] * 6 + [sspec],
             out_specs=[vspec] * 4,
-            scratch_shapes=[vm(6, NZ, NX, W), vm(NZ, NX, W), vm(2, NZ, NX, W)]
+            scratch_shapes=[vm(NZ, NX, W)] * 5 + [pltpu.VMEM((NZ, NX, W), jnp.int32)]
+            + [vm(6, NZ, NX, W), vm(NZ, NX, W), vm(2, NZ, NX, W)]
             + layers() + layers()
             + [vm(2, NZ, W), vm(2, NX, W), vm(2, NX, W),
-               vm(2, NZ, NX, W), vm(GY, 2, NZ, R, W), vm(GY, NZ, W), vm(GY, NZ, W),
-               dma((6 * T,)), dma((6 * T,)), dma((GY,)), dma((GY,)), dma((GY + 1,)), dma((GY,))],
+               vm(NB, 2, ZC, NX, W), vm(NB, GY, 2, ZC, R, W), vm(NB, GY, ZC, W), vm(NB, GY, ZC, W),
+               vm(NB, 2 * ZC, W), vm(NB, 2 * ZC, W), vm(NB, NX, W), vm(NB, NX, W),
+               dma((6,)), dma((6 * T,)), dma((6 * T,)), dma((NB * GY,)), dma((NB * GY,)),
+               dma((NB * (GY + 1),)), dma((NB * GY,)), dma((2 * NB,)), dma((2 * NB,))],
             compiler_params=pltpu.CompilerParams(
-                collective_id=0, has_side_effects=True, vmem_limit_bytes=48 * 1024 * 1024),
+                collective_id=0, has_side_effects=True, vmem_limit_bytes=60 * 1024 * 1024),
         )(o_r, o_i, p_z, p_x, p_y, mat, lev)
 
     block = P("gz", "gx", "gy")

time: 48.1 us -> 40.4 us (0.84)
  local copies, waits for them, and re-layouts: 10.1 us -> 5.2 us
  Pallas kernels: 37 us -> 34 us
    unnamed x18 -> x10, local copies, waits for them, and re-layouts: 10.1 us -> 5.2 us
    pallas_call x1, Pallas kernels: 37 us -> 34 us  [shards(): pl.pallas_call(functools.partial(kernel, (NZ, NX, R, GX, GY, GZ)), out_sh...]
where the time goes in v2:
time: 40.4 us; the launch traced here: 39.8 us
  Pallas kernels  34 us (84%)
  local copies, waits for them, and re-layouts  5.2 us (13%)
  between operations  0.65 us (2%)
    pallas_call x1, Pallas kernels, shards(): pl.pallas_call(functools.partial(kernel, (NZ, NX, R, GX, GY, GZ)), out_sh...  34 us
    unnamed x10, local copies, waits for them, and re-layouts  5.2 us

profile of v2, /device:TPU:0, one launch (start us, length us, event | category | flops | bytes accessed | tf_op | source)
XLA Modules:
  0.0 39.8 jit_solution(6074461643855014874)
XLA Ops:
  0.6 34.0 %shard_map.102 = (f32[16,64,128]{2,1,0:T(8,128)}, f32[16,64,128]{2,1,0:T(8,128)}, f32[16,16,512]{2,1,0:T(8,128)}, f32[16,16,512]{2,1,0:T(8,128)}) custom-call(f32[16,64,128]{2,1,0:T(8,128)} %h0.1, f32[16,64,128]{2,1,0:T(8,128)} %h1.1, f32[16,64,128]{2,1,0:T(8,128)} %h2.1, f32[16,64,128]{2,1,0:T(8,128)} %h3.1, f32[16,64,128]{2,1,0:T(8,128)} %h4.1, ...), custom_call_target="tpu_custom_call" | custom-call | tf_op jit(solution)/shard_map/pallas_call | solution.py:398
  34.6 0.0 copy-start.2
  34.6 1.9 %copy.15 = f32[16,64,128]{2,1,0:T(8,128)} copy(f32[16,64,128]{2,1,0:T(8,128)} %get-tuple-element.8) | data formatting | bytes 1048576
  36.6 0.0 copy-done.2
  36.6 0.0 copy-start.1
  36.6 0.8 %copy.16 = f32[16,64,128]{2,1,0:T(8,128)} copy(f32[16,64,128]{2,1,0:T(8,128)S(1)} %copy-done.2) | data formatting | bytes 1048576
  37.4 0.4 %copy-done.1 = f32[16,16,512]{2,1,0:T(8,128)S(1)} copy-done((f32[16,16,512]{2,1,0:T(8,128)S(1)}, f32[16,16,512]{2,1,0:T(8,128)}, u32[]{:S(2)}) %copy-start.1) | copy-done | bytes 524312
  37.8 0.0 copy-start
  37.8 0.8 %copy.17 = f32[16,16,512]{2,1,0:T(8,128)} copy(f32[16,16,512]{2,1,0:T(8,128)S(1)} %copy-done.1) | data formatting | bytes 1048576
  38.6 0.4 %copy-done = f32[16,16,512]{2,1,0:T(8,128)S(1)} copy-done((f32[16,16,512]{2,1,0:T(8,128)S(1)}, f32[16,16,512]{2,1,0:T(8,128)}, u32[]{:S(2)}) %copy-start) | copy-done | bytes 524312
  39.0 0.8 %copy.18 = f32[16,16,512]{2,1,0:T(8,128)} copy(f32[16,16,512]{2,1,0:T(8,128)S(1)} %copy-done) | data formatting | bytes 1048576
Async XLA Ops:
  34.6 2.0 %copy-start.2 = (f32[16,64,128]{2,1,0:T(8,128)S(1)}, f32[16,64,128]{2,1,0:T(8,128)}, u32[]{:S(2)}) copy-start(f32[16,64,128]{2,1,0:T(8,128)} %get-tuple-element.9) | copy-start | bytes 1572868
  36.6 1.2 %copy-start.1 = (f32[16,16,512]{2,1,0:T(8,128)S(1)}, f32[16,16,512]{2,1,0:T(8,128)}, u32[]{:S(2)}) copy-start(f32[16,16,512]{2,1,0:T(8,128)} %get-tuple-element.10) | copy-start | bytes 1572868
  37.8 1.2 %copy-start = (f32[16,16,512]{2,1,0:T(8,128)S(1)}, f32[16,16,512]{2,1,0:T(8,128)}, u32[]{:S(2)}) copy-start(f32[16,16,512]{2,1,0:T(8,128)} %get-tuple-element.11) | copy-start | bytes 1572868

commit v3 on v2

--- a/solution.py
+++ b/solution.py
@@ -48,11 +48,11 @@
     return acc
 
 
-def kernel(dims, h0, h1, h2, h3, h4, h5, lev, fr, fi, circ, flux,
-           o_r, o_i, p_z, p_x, p_y, mat, cs, eps, st, zu_s, zd_s, xu_s, xd_s, yu_s, yd_s,
+def kernel(dims, h0, h1, h2, h3, h4, h5, lev, g0, g1, g2, g3,
+           fr, fi, circ, flux, o_r, o_i, p_z, p_x, p_y, mat, cs, eps, st, zu_s, zd_s, xu_s, xd_s, yu_s, yd_s,
            zu_r, zd_r, xu_r, xd_r, yu_r, yd_r, ecx, ecy, ecz,
            jj, rj, e_s, e_r, fx_s, fx_r, fy_s, fy_r,
-           insem, snd, rcv, jsnd, jrcv, esnd, ercv, fsnd, frcv):
+           insem, outsem, snd, rcv, jsnd, jrcv, esnd, ercv, fsnd, frcv):
     NZ, NX, R, GX, GY, GZ = dims
     gx, gy, gz = (lax.axis_index(a) for a in ("gx", "gy", "gz"))
     lane = iota((NX, W), 1)
@@ -352,6 +352,13 @@
             circ[zs, :, s * W:(s + 1) * W] = (
                 (jx[s] - j_x_next).reshape(ZC, R, W) + j_y_next - j_y)
 
+    def store(b, n, src, dst):
+        zs = pl.ds(b * ZC, ZC)
+        return pltpu.make_async_copy(src.at[zs], dst.at[zs], outsem.at[4 * b + n])
+
+    outs = [[store(b, n, src, dst) for n, (src, dst) in enumerate(
+        ((fr, g0), (fi, g1), (circ, g2), (flux, g3)))] for b in range(NB)]
+
     arrive(rounds[1])
     second = step(1, s_r, s_i, fr, fi)
     carry = (zu_r[1, 0], zu_r[1, 1])
@@ -360,6 +367,8 @@
             carry = second(b * ZC, (b + 1) * ZC, carry)
             faces(b)
             launch(final[b])
+            outs[b][0].start()
+            outs[b][1].start()
         if b > 0:
             arrive(final[b - 1])
             currents(b - 1)
@@ -367,15 +376,33 @@
     for b in range(NB):
         receive(b)
         slab(b)
+        outs[b][2].start()
+        outs[b][3].start()
 
     for msgs in rounds + final:
         for copy, scond, _, _ in msgs:
             pl.when(scond)(copy.wait_send)
     for b in range(NB):
+        for copy in outs[b]:
+            copy.wait()
         for k in range(1, G):
             slab_copy(b, k).wait_send()
             pl.when(lax.rem(gy + k, G) != G - 1)(row_copy(b, k).wait_send)
         pl.when(gx > 0)(last_row_copy(b, 0).wait_send)
+
+
+def place(*refs):
+    n = (len(refs) - 2) // 3
+    src, dst, mid, insem, outsem = refs[:n], refs[n:2 * n], refs[2 * n:3 * n], refs[-2], refs[-1]
+    loads = [pltpu.make_async_copy(src[k], mid[k], insem.at[k]) for k in range(n)]
+    saves = [pltpu.make_async_copy(mid[k], dst[k], outsem.at[k]) for k in range(n)]
+    for load in loads:
+        load.start()
+    for load, save in zip(loads, saves):
+        load.wait()
+        save.start()
+    for save in saves:
+        save.wait()
 
 
 def solution(mesh):
@@ -389,29 +416,35 @@
         T = STEPS
         NB = NZ // ZC
         vm = lambda *shape: pltpu.VMEM(shape, f32)
-        vspec = pl.BlockSpec(memory_space=pltpu.VMEM)
         hspec = pl.BlockSpec(memory_space=pl.ANY)
         sspec = pl.BlockSpec(memory_space=pltpu.SMEM)
         dma = pltpu.SemaphoreType.DMA
         layers = lambda: [vm(T, 2, NX, W), vm(T, 2, NX, W), vm(T, 2, NZ, W), vm(T, 2, NZ, W),
                           vm(T, NX, W), vm(T, NX, W)]
-        return pl.pallas_call(
+        shapes = ([jax.ShapeDtypeStruct((NZ, NX, W), f32)] * 2
+                  + [jax.ShapeDtypeStruct((NZ, R, GY * W), f32)] * 2)
+        bufs = [vm(*shape.shape) for shape in shapes]
+        results = pl.pallas_call(
             functools.partial(kernel, (NZ, NX, R, GX, GY, GZ)),
-            out_shape=[jax.ShapeDtypeStruct((NZ, NX, W), f32)] * 2
-            + [jax.ShapeDtypeStruct((NZ, R, GY * W), f32)] * 2,
+            out_shape=shapes,
             in_specs=[hspec] * 6 + [sspec],
-            out_specs=[vspec] * 4,
-            scratch_shapes=[vm(NZ, NX, W)] * 5 + [pltpu.VMEM((NZ, NX, W), jnp.int32)]
+            out_specs=[hspec] * 4,
+            scratch_shapes=bufs + [vm(NZ, NX, W)] * 5 + [pltpu.VMEM((NZ, NX, W), jnp.int32)]
             + [vm(6, NZ, NX, W), vm(NZ, NX, W), vm(2, NZ, NX, W)]
             + layers() + layers()
             + [vm(2, NZ, W), vm(2, NX, W), vm(2, NX, W),
                vm(NB, 2, ZC, NX, W), vm(NB, GY, 2, ZC, R, W), vm(NB, GY, ZC, W), vm(NB, GY, ZC, W),
                vm(NB, 2 * ZC, W), vm(NB, 2 * ZC, W), vm(NB, NX, W), vm(NB, NX, W),
-               dma((6,)), dma((6 * T,)), dma((6 * T,)), dma((NB * GY,)), dma((NB * GY,)),
+               dma((6,)), dma((4 * NB,)), dma((6 * T,)), dma((6 * T,)), dma((NB * GY,)), dma((NB * GY,)),
                dma((NB * (GY + 1),)), dma((NB * GY,)), dma((2 * NB,)), dma((2 * NB,))],
             compiler_params=pltpu.CompilerParams(
                 collective_id=0, has_side_effects=True, vmem_limit_bytes=60 * 1024 * 1024),
         )(o_r, o_i, p_z, p_x, p_y, mat, lev)
+        return pl.pallas_call(
+            place, out_shape=shapes, in_specs=[hspec] * 4, out_specs=[hspec] * 4,
+            scratch_shapes=bufs + [dma((4,)), dma((4,))],
+            compiler_params=pltpu.CompilerParams(vmem_limit_bytes=60 * 1024 * 1024),
+        )(*results)
 
     block = P("gz", "gx", "gy")
     line = P("gz", ("gx", "gy"), None)

time: 40.4 us -> 36.9 us (0.913)
  local copies, waits for them, and re-layouts: 5.2 us -> 0 us
  Pallas kernels: 34 us -> 35.8 us
    unnamed x10 -> x0, local copies, waits for them, and re-layouts: 5.2 us -> none
    pallas_call x0 -> x1, Pallas kernels: none -> 2.42 us  [shards(): pl.pallas_call(place, out_shape=shapes, in_specs=[hspec] * 4, out_specs=[...]
    pallas_call x1, Pallas kernels: 34 us -> 33.4 us  [shards(): pl.pallas_call(functools.partial(kernel, (NZ, NX, R, GX, GY, GZ)), out_sh...]
where the time goes in v3:
time: 36.9 us; the launch traced here: 36.5 us
  Pallas kernels  35.8 us (97%)
  between operations  0.64 us (2%)
    pallas_call x1, Pallas kernels, shards(): pl.pallas_call(functools.partial(kernel, (NZ, NX, R, GX, GY, GZ)), out_sh...  33.4 us
    pallas_call x1, Pallas kernels, shards(): pl.pallas_call(place, out_shape=shapes, in_specs=[hspec] * 4, out_specs=[...  2.42 us

profile of v3, /device:TPU:0, one launch (start us, length us, event | category | flops | bytes accessed | tf_op | source)
XLA Modules:
  0.0 36.5 jit_solution(2000369114562921504)
XLA Ops:
  0.6 33.4 %shard_map.102 = (f32[16,64,128]{2,1,0:T(8,128)}, f32[16,64,128]{2,1,0:T(8,128)}, f32[16,16,512]{2,1,0:T(8,128)}, f32[16,16,512]{2,1,0:T(8,128)}) custom-call(f32[16,64,128]{2,1,0:T(8,128)} %h0.1, f32[16,64,128]{2,1,0:T(8,128)} %h1.1, f32[16,64,128]{2,1,0:T(8,128)} %h2.1, f32[16,64,128]{2,1,0:T(8,128)} %h3.1, f32[16,64,128]{2,1,0:T(8,128)} %h4.1, ...), custom_call_target="tpu_custom_call" | custom-call | tf_op jit(solution)/shard_map/pallas_call | solution.py:427
  34.0 2.4 %shard_map.103 = (f32[16,64,128]{2,1,0:T(8,128)}, f32[16,64,128]{2,1,0:T(8,128)}, f32[16,16,512]{2,1,0:T(8,128)}, f32[16,16,512]{2,1,0:T(8,128)}) custom-call(f32[16,64,128]{2,1,0:T(8,128)} %get-tuple-element.8.refs_0_, f32[16,64,128]{2,1,0:T(8,128)} %get-tuple-element.9.refs_1_, f32[16,16,512]{2,1,0:T(8,128)} %get-tuple-element.10.refs_2_, ...), custom_call_target="tpu_custom_call" | custom-call | tf_op jit(solution)/shard_map/pallas_call | solution.py:443
